TPU v7x, 256 devices: a whole 4x4x8 slice. The times are simulated.
256 devices in a mesh: tm: 16 (over y_lo, x, core), blk: 8 (over z), samp: 2 (over y_hi).
Axes of the slice: x: 4, y: 4 (y_hi: 2, y_lo: 2; y = y_hi * 2 + y_lo), z: 8, core: 2. Of those that a mesh axis runs over, the one named last changes fastest.
Arguments:
- prior_path: float32 [32, 16, 1024], P('tm', 'samp', 'blk'), may hold values from -6 to 6
- observed: float32 [32, 256], P('tm', 'blk'), may hold values from -6 to 6
- obs_mask: int32 [32, 32], P('tm', 'blk'), may hold values 0 or 1
- noise_draw: float32 [32, 16, 256], P('tm', 'samp', 'blk'), may hold values from -6 to 6
- wend_blocks: float32 [128, 8, 8], P('blk'), may hold values from -1 to 1
- block_cols: int32 [128], P('blk'), may hold values from 0 to 31, as said below
- start_mean: float32 [16, 1024], P('samp', 'blk'), may hold values from -6 to 6
- trans_mats: bfloat16 [32, 1024, 1024], P('tm', 'blk', 'samp')
- gain_mats: bfloat16 [32, 1024, 256], P('tm', 'blk', 'samp'), may hold values from -0.375 to 0.375
- smooth_mats: bfloat16 [32, 1024, 1024], P('tm', 'blk', 'samp')
- site_trans: float32 [4, 4], replicated, may hold values from -2.5 to 2.5
Outputs:
- posterior_path: float32 [32, 16, 1024], P('tm', 'samp', 'blk')
Inputs may be any that keep to these rules, and one draw needn't show every extreme that they name: `block_cols`: entry 4 i names block i itself, entries 4 i + 1 to 4 i + 3 name three different blocks among i - 2, i - 1, i + 1, i + 2 taken modulo 32.
All inputs are finite; a program needn't handle non-finite values. No bound on the sum of `obs_mask` on one device may be relied on, other than what follows from the above.
Results may differ from a plain program's by a relative error of at most 0.0003.
Values may be sent and summed in bfloat16 or wider, within the bound.
No kernel may reach another device: no remote copies, remote signals or barrier semaphores. Data moves between devices by JAX's collectives and lax.ppermute only.
A program may use at most 64 MiB of HBM per device.

v0:
```python
import functools
import jax
import jax.numpy as jnp
from jax import lax
from jax.experimental import pallas as pl
from jax.experimental.pallas import tpu as pltpu
from jax.sharding import PartitionSpec as P

highest = lax.Precision.HIGHEST
bf16, f32 = jnp.bfloat16, jnp.float32
ROWS_BY_ROWS = (((1,), (1,)), ((), ()))
VMEM_LIMIT = 2 * 1024 * 1024


def ring(count, step):
    return [(i, (i + step) % count) for i in range(count)]


def swapped(count):
    return [(i, i ^ 1) for i in range(count)]


def all_blocks(value, axis):
    count = lax.axis_size(axis)
    copies = jnp.broadcast_to(value[None], (count,) + value.shape)
    return lax.all_to_all(copies, axis, 0, 0, tiled=True)


def observation_noise(noise_draw, wend_blocks, block_cols):
    step_count, sample_count, local_sites = noise_draw.shape
    block_sites = wend_blocks.shape[1]
    local_blocks = local_sites // block_sites
    cycle = lax.axis_size("blk")
    rim = 2 * block_sites
    before = lax.ppermute(noise_draw[:, :, local_sites - rim :], "blk", ring(cycle, 1))
    after = lax.ppermute(noise_draw[:, :, :rim], "blk", ring(cycle, -1))
    widened = jnp.concatenate([before, noise_draw, after], axis=2)
    pair_rows = jnp.arange(local_blocks * 4, dtype=jnp.int32) // 4
    first_block = lax.axis_index("blk") * local_blocks
    offset = (block_cols - first_block - pair_rows + 2) % (local_blocks * cycle)
    chooser = (
        (pair_rows + offset)[:, None] == jnp.arange(local_blocks + 4, dtype=jnp.int32)[None, :]
    ).astype(f32)
    blocks = wend_blocks.reshape(local_blocks, 4, block_sites, block_sites)
    chooser = chooser.reshape(local_blocks, 4, local_blocks + 4)
    mixer = jnp.sum(chooser[:, :, :, None, None] * blocks[:, :, None, :, :], axis=1)
    mixer = mixer.transpose(1, 3, 0, 2).reshape(local_sites + 2 * rim, local_sites)
    return jnp.einsum("tsl,lm->tsm", widened, mixer, precision=highest)


def split_rows(value):
    high = value.astype(bf16)
    rest = value - high.astype(f32)
    middle = rest.astype(bf16)
    low = (rest - middle.astype(f32)).astype(bf16)
    return jnp.concatenate([high, middle, low], axis=0)


def joined_rows(value):
    rows = value.shape[0] // 3
    return value[:rows] + value[rows : 2 * rows] + value[2 * rows :]


def start_copies(shards, out_ref, sems, used, owner, side):
    width = shards.shape[3]
    columns = pl.ds(pl.multiple_of(side * width, 128), width)
    copies = []
    for step in range(shards.shape[1]):
        target = out_ref.at[owner * shards.shape[1] + step, :, :, columns]
        copy = pltpu.make_async_copy(shards.at[:, step], target, sems.at[used + step])
        copy.start()
        copies.append(copy)
    return copies


def pack_ring_kernel(count, place, near, far, *refs):
    shards, out_ref, sems = refs[: 2 * count], refs[2 * count], refs[2 * count + 1]
    blk, samp, core = place[0], place[1], place[2]
    copies = start_copies(near, out_ref, sems, 0, core, samp)
    copies += start_copies(far, out_ref, sems, 2, 1 - core, samp)
    for n, shard in enumerate(shards):
        whose, k = n // count, n % count
        steps, rows, width = shard.shape
        owner = core if whose == 0 else 1 - core
        at = lax.rem(blk - k + count, count)
        columns = pl.ds(pl.multiple_of((1 - samp) * width, 128), width)
        target = out_ref.at[pl.ds(owner * steps, steps), at, :, columns]
        copy = pltpu.make_async_copy(shard, target, sems.at[4 + n])
        copy.start()
        copies.append(copy)
    for copy in copies:
        copy.wait()


def pack_kernel(place, near, far, out_ref, sems):
    samp, core = place[1], place[2]
    copies = []
    for whose, shards in enumerate((near, far)):
        owner = core if whose == 0 else 1 - core
        for half in range(2):
            side = samp if half == 0 else 1 - samp
            copies += start_copies(shards.at[:, half], out_ref, sems, len(copies), owner, side)
    for copy in copies:
        copy.wait()


def apply_rows(mats, turn, value, store):
    count, rows, _ = mats.shape[1:]
    terms = split_rows(value)
    for k in range(0, count, 2):
        block = jnp.concatenate([mats[turn, k], mats[turn, k + 1]], axis=0)
        part = lax.dot_general(terms, block, ROWS_BY_ROWS, preferred_element_type=f32)
        store(slice(k * rows, (k + 2) * rows), joined_rows(part))


def forward_kernel(hop, place, state_ref, near_in, far_in, mats, *refs):
    filt_ref, sent_ref = refs[-2:]

    @pl.when(place[3] == hop)
    def _():
        sent_ref[...] = state_ref[...]

        def step(turn, carry):
            is_near = turn // 2 == place[2]

            def store(columns, part):
                at = lax.rem(turn, 2)
                added = jnp.where(is_near, near_in[at, :, columns], far_in[at, :, columns])
                filt_ref[turn, :, columns] = part + added

            apply_rows(mats, turn, sent_ref[...], store)
            sent_ref[...] = filt_ref[turn]
            return carry

        lax.fori_loop(0, 4, step, 0)


def backward_kernel(hop, hops, place, state_ref, filt_ref, pred_ref, mats, *refs):
    target_ref, sent_ref = refs[-2:]

    @pl.when(place[3] == hop)
    def _():
        sent_ref[...] = state_ref[...]

        def step(i, carry):
            turn = 3 - i
            change = sent_ref[...] - pred_ref[turn]
            if hop == hops - 1:
                change = jnp.where(turn == 3, 0.0, change)

            def store(columns, part):
                target_ref[turn, :, columns] = filt_ref[turn, :, columns] + part

            apply_rows(mats, turn, change, store)
            sent_ref[...] = target_ref[turn]
            return carry

        lax.fori_loop(0, 4, step, 0)


def finish_kernel(place, prior_ref, smooth_ref, out_ref):
    width = out_ref.shape[2]
    columns = pl.ds(pl.multiple_of(place[0] * width, 128), width)
    for step in range(2):
        out_ref[step] = prior_ref[step] + smooth_ref[place[2] * 2 + step, :, columns]


def predict_kernel(site_ref, filt_ref, out_ref):
    steps, samples, states = filt_ref.shape
    width = 128
    row = lax.broadcasted_iota(jnp.int32, (width, width), 0)
    column = lax.broadcasted_iota(jnp.int32, (width, width), 1)
    same_site = row // 4 == column // 4
    kron = jnp.zeros((width, width), f32)
    for i in range(4):
        for j in range(4):
            here = same_site & (row % 4 == i) & (column % 4 == j)
            kron = jnp.where(here, site_ref[i, j], kron)
    for k in range(0, states, width):
        rows = filt_ref[:, :, k : k + width].reshape(steps * samples, width)
        moved = lax.dot_general(
            rows, kron, ROWS_BY_ROWS, precision=highest, preferred_element_type=f32
        )
        out_ref[:, :, k : k + width] = moved.reshape(steps, samples, width)


SMEM = pl.BlockSpec(memory_space=pltpu.SMEM)
VMEM = pl.BlockSpec(memory_space=pltpu.VMEM)
ANY = pl.BlockSpec(memory_space=pl.ANY)
HBM = pl.BlockSpec(memory_space=pltpu.HBM)


def call(kernel, name, shapes, specs, scratch=(), aliases=None):
    return pl.pallas_call(
        kernel,
        out_shape=shapes,
        in_specs=specs,
        out_specs=jax.tree.map(lambda _: VMEM, shapes),
        scratch_shapes=list(scratch),
        input_output_aliases=aliases or {},
        compiler_params=pltpu.CompilerParams(vmem_limit_bytes=VMEM_LIMIT),
        name=name,
    )


def in_vmem(value):
    return pltpu.with_memory_space_constraint(value, pltpu.VMEM)


def on_device(
    prior_path,
    observed,
    obs_mask,
    noise_draw,
    wend_blocks,
    block_cols,
    start_mean,
    trans_mats,
    gain_mats,
    smooth_mats,
    site_trans,
):
    cycle, times = lax.axis_size("blk"), lax.axis_size("tm")
    blk, samp, time = lax.axis_index("blk"), lax.axis_index("samp"), lax.axis_index("tm")
    groups = times // 2
    group, core = time // 2, time % 2
    step_count, sample_count, local_sites = noise_draw.shape
    block_sites = wend_blocks.shape[1]
    state_count = trans_mats.shape[1] * cycle
    cores = swapped(times)
    place = jnp.stack([blk, samp, core, group]).astype(jnp.int32)

    trans_other = lax.ppermute(trans_mats, "samp", swapped(2))
    near = lax.all_gather(jnp.stack([trans_mats, trans_other]), "blk", axis=0)

    obs_noise = observation_noise(noise_draw, wend_blocks, block_cols)
    first_comp = prior_path.reshape(step_count, sample_count, local_sites, 4)[:, :, :, 0]
    seen_mask = jnp.repeat(obs_mask.astype(f32), block_sites, axis=1)
    residual = seen_mask[:, None, :] * (observed[:, None, :] - first_comp - obs_noise)
    all_resid = all_blocks(residual, "blk").transpose(1, 2, 0, 3)
    all_resid = all_resid.reshape(step_count, sample_count, local_sites * cycle)
    gain_other = lax.ppermute(gain_mats, "samp", swapped(2))
    gain = jnp.where(
        samp == 0,
        jnp.concatenate([gain_mats, gain_other], axis=2),
        jnp.concatenate([gain_other, gain_mats], axis=2),
    )
    inputs = jnp.einsum("tij,tsj->tsi", gain, all_resid, precision=highest)
    gathered = all_blocks(jnp.concatenate([inputs, start_mean[None]], axis=0), "blk")
    gathered = gathered.transpose(1, 2, 0, 3).reshape(step_count + 1, sample_count, state_count)
    near_in, start = gathered[:step_count], gathered[step_count]
    far_in = lax.ppermute(near_in, "tm", cores)
    mats_shape = jax.ShapeDtypeStruct((4, cycle, trans_mats.shape[1], state_count), bf16)

    def pack(value, name):
        far = lax.ppermute(value, "tm", cores)
        dmas = [pltpu.SemaphoreType.DMA((8,))]
        return in_vmem(call(pack_kernel, name, mats_shape, [SMEM, HBM, HBM], dmas)(place, value, far))

    near, near_in = lax.optimization_barrier((near, near_in))
    trans = pack(near, "pack_trans")

    smooth_mats, _ = lax.optimization_barrier((smooth_mats, all_resid))
    smooth_other = lax.ppermute(smooth_mats, "samp", swapped(2))
    near_smooth = lax.all_gather(jnp.stack([smooth_mats, smooth_other]), "blk", axis=0)

    filt_shape = jax.ShapeDtypeStruct((4, sample_count, state_count), f32)
    state_shape = jax.ShapeDtypeStruct((sample_count, state_count), f32)

    def forward(hop, state, *filtered):
        return call(
            functools.partial(forward_kernel, hop),
            "forward",
            (filt_shape, state_shape),
            [SMEM] + [VMEM] * (4 + len(filtered)),
            (),
            {5: 0} if filtered else None,
        )(place, state, near_in, far_in, trans, *filtered)

    filtered, sent = forward(0, start)
    for hop in range(1, groups):
        pairs = [(2 * hop - 2, 2 * hop), (2 * hop - 1, 2 * hop + 1)]
        state = lax.ppermute(sent, "tm", pairs)
        if hop == groups - 1:
            near_smooth, filtered = lax.optimization_barrier((near_smooth, filtered))
            smooth = pack(near_smooth, "pack_smooth")
            filtered, smooth = lax.optimization_barrier((filtered, smooth))
        filtered, sent = forward(hop, state, filtered)

    predicted = call(predict_kernel, "predict", filt_shape, [SMEM, VMEM])(site_trans, filtered)

    def backward(hop, state, *smoothed):
        return call(
            functools.partial(backward_kernel, hop, groups),
            "backward",
            (filt_shape, state_shape),
            [SMEM] + [VMEM] * (4 + len(smoothed)),
            (),
            {5: 0} if smoothed else None,
        )(place, state, filtered, predicted, smooth, *smoothed)

    smoothed, sent = backward(groups - 1, sent)
    for hop in range(groups - 2, -1, -1):
        pairs = [(2 * hop + 2, 2 * hop), (2 * hop + 3, 2 * hop + 1)]
        state = lax.ppermute(sent, "tm", pairs)
        smoothed, sent = backward(hop, state, smoothed)
    out_shape = jax.ShapeDtypeStruct(prior_path.shape, f32)
    return call(finish_kernel, "finish", out_shape, [SMEM, VMEM, VMEM])(place, prior_path, smoothed)


def solution(mesh):
    placed = (
        P("tm", "samp", "blk"),
        P("tm", "blk"),
        P("tm", "blk"),
        P("tm", "samp", "blk"),
        P("blk", None, None),
        P("blk"),
        P("samp", "blk"),
        P("tm", "blk", "samp"),
        P("tm", "blk", "samp"),
        P("tm", "blk", "samp"),
        P(),
    )
    return jax.shard_map(
        on_device, mesh=mesh, in_specs=placed, out_specs=P("tm", "samp", "blk"), check_vma=False
    )
```

profile of v0, /device:TPU:16, one launch (start us, length us, event | category | flops | bytes accessed | tf_op | source)
XLA Modules:
  0.0 223.2 jit_solution(624237714065847319)
XLA Ops:
  6.5 2.1 collective-permute-start.3
  8.6 7.7 %collective-permute-done.3 = bf16[2,128,512]{2,1,0:T(8,128)(2,1)S(1)} collective-permute-done((bf16[2,128,512]{2,1,0:T(8,128)(2,1)}, bf16[2,128,512]{2,1,0:T(8,128)(2,1)S(1)}, u32[]{:S(2)}, u32[]{:S(2)}) %collective-permute-start.3) | collective-permute-done | bytes 262176 | tf_op jit(solution)/shard_map/ppermute | solution.py:233
  16.3 1.8 pad_maximum_fusion
  19.0 1.9 collective-permute-start
  20.9 4.0 %collective-permute-start.1 = (f32[2,8,16]{2,1,0:T(8,128)S(1)}, f32[2,8,16]{2,1,0:T(8,128)S(1)}, u32[]{:S(2)}, u32[]{:S(2)}) collective-permute-start(f32[2,8,16]{2,1,0:T(8,128)S(1)} %get-tuple-element.82), channel_id=1, source_target_pairs={{0,14},{2,0},{4,2},{6,4},{8,6},{10,8},{12,10},{14,12},{1,15},{3,1}... | collective-permute-start | bytes 3080 | tf_op jit(solution)/shard_map/ppermute | solution.py:36
  29.7 13.6 %all_to_all.10 = f32[8,1,512]{2,1,0:T(1,128)S(1)} all-to-all(f32[8,1,512]{2,1,0:T(1,128)S(1)} %reshape.39), channel_id=1, replica_groups=mesh['tm'=16,'blk'=8,'samp'=2] {'blk'}, dimensions={0} | all-to-all | bytes 32768 | tf_op jit(solution)/shard_map/all_to_all | solution.py:26
  45.2 7.8 %collective-permute-done.13 = bf16[2,128,512]{2,1,0:T(8,128)(2,1)S(1)} collective-permute-done((bf16[2,128,512]{2,1,0:T(8,128)(2,1)}, bf16[2,128,512]{2,1,0:T(8,128)(2,1)S(1)}, u32[]{:S(2)}, u32[]{:S(2)}) %collective-permute-start.13) | collective-permute-done | bytes 262176 | tf_op jit(solution)/shard_map/ppermute | solution.py:264
  52.9 1.8 pad_maximum_fusion.1
  55.2 5.4 %collective-permute-done.2 = bf16[2,128,128]{2,1,0:T(8,128)(2,1)S(1)} collective-permute-done((bf16[2,128,128]{2,1,0:T(8,128)(2,1)S(1)}, bf16[2,128,128]{2,1,0:T(8,128)(2,1)S(1)}, u32[]{:S(2)}, u32[]{:S(2)}) %collective-permute-start.2) | collective-permute-done | bytes 65568 | tf_op jit(solution)/shard_map/ppermute | solution.py:242
  60.9 12.1 %all_to_all.11 = f32[8,3,8,128]{3,2,1,0:T(8,128)S(1)} all-to-all(f32[8,3,8,128]{3,2,1,0:T(8,128)S(1)} %broadcast_in_dim.11), channel_id=1, replica_groups=mesh['tm'=16,'blk'=8,'samp'=2] {'blk'}, dimensions={0} | all-to-all | bytes 196608 | tf_op jit(solution)/shard_map/all_to_all | solution.py:26
  73.0 5.4 %all-gather.5.cloned.1.call-done = bf16[16,2,128,512]{3,2,1,0:T(8,128)(2,1)} async-done(((bf16[2,2,128,512]{3,2,1,0:T(8,128)(2,1)}), bf16[16,2,128,512]{3,2,1,0:T(8,128)(2,1)}) %all-gather.5.cloned.1.call-update) | async-done | bytes 4194320 | tf_op jit(solution)/shard_map/all_gather | solution.py:234
  79.0 7.0 %collective-permute-done.5.far = bf16[8,2,2,128,512]{4,3,2,1,0:T(8,128)(2,1)} collective-permute-done((bf16[8,2,2,128,512]{4,3,2,1,0:T(8,128)(2,1)}, bf16[8,2,2,128,512]{4,3,2,1,0:T(8,128)(2,1)}, u32[]{:S(2)}, u32[]{:S(2)}) %collective-permute-start.5) | collective-permute-done | bytes 4194336 | tf_op jit(solution)/shard_map/ppermute | solution.py:256
  86.0 2.2 copy-done.3
  88.2 3.6 %pack_trans.1.mats = bf16[4,8,128,1024]{3,2,1,0:T(8,128)(2,1)S(1)} custom-call(s32[4]{0:T(128)S(1)} %pad_add_fusion.place, bf16[8,2,2,128,512]{4,3,2,1,0:T(8,128)(2,1)S(1)} %bitcast.35, bf16[8,2,2,128,512]{4,3,2,1,0:T(8,128)(2,1)} %collective-permute-done.5.far), custom_call_target="tpu_custom_call" | custom-call | tf_op jit(solution)/shard_map/pack_trans/pallas_call | solution.py:258
  91.8 3.5 %forward.8 = (f32[4,8,1024]{2,1,0:T(8,128)S(1)}, f32[8,1024]{1,0:T(8,128)S(1)}) custom-call(s32[4]{0:T(128)S(1)} %pad_add_fusion.place, f32[8,1024]{1,0:T(8,128)S(1)} %slice_bitcast_fusion.state_ref, f32[2,8,1024]{2,1,0:T(8,128)S(1)} %copy_bitcast_fusion.near_in, f32[2,8,1024]{2,1,0:T(8,128)S(1)} %collective-permute-done.4.far_in, ...), custom_call_target="tpu_custom_call" | custom-call | tf_op jit(solution)/shard_map/forward/pallas_call | solution.py:271
  96.6 1.6 collective-permute-done.6.state_ref
  105.0 28.7 %all-gather.7.cloned.1.call-done = bf16[16,2,128,512]{3,2,1,0:T(8,128)(2,1)} async-done(((bf16[2,2,128,512]{3,2,1,0:T(8,128)(2,1)}), bf16[16,2,128,512]{3,2,1,0:T(8,128)(2,1)}) %all-gather.7.cloned.1.call-update) | async-done | bytes 4194320 | tf_op jit(solution)/shard_map/all_gather | solution.py:265
  134.3 6.7 %collective-permute-done.14.far = bf16[8,2,2,128,512]{4,3,2,1,0:T(8,128)(2,1)S(1)} collective-permute-done((bf16[8,2,2,128,512]{4,3,2,1,0:T(8,128)(2,1)}, bf16[8,2,2,128,512]{4,3,2,1,0:T(8,128)(2,1)S(1)}, u32[]{:S(2)}, u32[]{:S(2)}) %collective-permute-start.14) | collective-permute-done | bytes 4194336 | tf_op jit(solution)/shard_map/ppermute | solution.py:256
  141.0 2.2 copy-done.2
  143.2 1.8 pack_smooth.1.mats
  145.0 1.5 copy-done.1
  147.2 1.5 predict.1.pred_ref
  158.2 53.0 %collective-permute-done.21.state_ref = f32[8,1024]{1,0:T(8,128)S(1)} collective-permute-done((f32[8,1024]{1,0:T(8,128)S(1)}, f32[8,1024]{1,0:T(8,128)S(1)}, u32[]{:S(2)}, u32[]{:S(2)}) %collective-permute-start.21) | collective-permute-done | bytes 32800 | tf_op jit(solution)/shard_map/ppermute | solution.py:305
  211.2 4.1 %backward.15 = (f32[4,8,1024]{2,1,0:T(8,128)S(1)}, f32[8,1024]{1,0:T(8,128)}) custom-call(s32[4]{0:T(128)S(1)} %pad_add_fusion.place, f32[8,1024]{1,0:T(8,128)S(1)} %collective-permute-done.21.state_ref, f32[4,8,1024]{2,1,0:T(8,128)S(1)} %get-tuple-element.64.filt_ref, f32[4,8,1024]{2,1,0:T(8,128)S(1)} %predict.1.pred_ref, ...), custom_call_target="tpu_custom_call", output_to_operand_aliasing={{0}: (5, {})} | custom-call | tf_op jit(solution)/shard_map/backward/pallas_call | solution.py:293
  (94 shorter events, 28.4 us)
Async XLA Ops:
  6.5 71.9 %all-gather.5.cloned.1.call-start = ((), (), s32[]{:S(2)}) async-start(), calls=%async_computation.2 | async-start | bytes 4718592 | tf_op jit(solution)/shard_map/all_gather | solution.py:234
  6.5 9.8 %collective-permute-start.3 = (bf16[2,128,512]{2,1,0:T(8,128)(2,1)}, bf16[2,128,512]{2,1,0:T(8,128)(2,1)S(1)}, u32[]{:S(2)}, u32[]{:S(2)}) collective-permute-start(bf16[2,128,512]{2,1,0:T(8,128)(2,1)} %param.18), channel_id=1, source_target_pairs={{0,1},{1,0},{2,3},{3,2},{4,5},{5,4},{6,7},{7,6},{8,9},{9,8},{10,11... | collective-permute-start | bytes 786440 | tf_op jit(solution)/shard_map/ppermute | solution.py:233
  18.1 115.5 %all-gather.7.cloned.1.call-start = ((), (), s32[]{:S(2)}) async-start(), calls=%async_computation.3 | async-start | bytes 4718592 | tf_op jit(solution)/shard_map/all_gather | solution.py:265
  19.0 9.7 %collective-permute-start = (f32[2,8,16]{2,1,0:T(8,128)S(1)}, f32[2,8,16]{2,1,0:T(8,128)S(1)}, u32[]{:S(2)}, u32[]{:S(2)}) collective-permute-start(f32[2,8,16]{2,1,0:T(8,128)S(1)} %get-tuple-element.81), channel_id=1, source_target_pairs={{0,2},{2,4},{4,6},{6,8},{8,10},{10,12},{12,14},{14,0},{1,3},{3,5},... | collective-permute-start | bytes 3080 | tf_op jit(solution)/shard_map/ppermute | solution.py:35
  20.9 7.8 %collective-permute-start.1 = (f32[2,8,16]{2,1,0:T(8,128)S(1)}, f32[2,8,16]{2,1,0:T(8,128)S(1)}, u32[]{:S(2)}, u32[]{:S(2)}) collective-permute-start(f32[2,8,16]{2,1,0:T(8,128)S(1)} %get-tuple-element.82), channel_id=1, source_target_pairs={{0,14},{2,0},{4,2},{6,4},{8,6},{10,8},{12,10},{14,12},{1,15},{3,1}... | collective-permute-start | bytes 3080 | tf_op jit(solution)/shard_map/ppermute | solution.py:36
  44.8 8.2 %collective-permute-start.13 = (bf16[2,128,512]{2,1,0:T(8,128)(2,1)}, bf16[2,128,512]{2,1,0:T(8,128)(2,1)S(1)}, u32[]{:S(2)}, u32[]{:S(2)}) collective-permute-start(bf16[2,128,512]{2,1,0:T(8,128)(2,1)} %param.20), channel_id=1, source_target_pairs={{0,1},{1,0},{2,3},{3,2},{4,5},{5,4},{6,7},{7,6},{8,9},{9,8},{10,11... | collective-permute-start | bytes 786440 | tf_op jit(solution)/shard_map/ppermute | solution.py:264
  54.8 5.9 %collective-permute-start.2 = (bf16[2,128,128]{2,1,0:T(8,128)(2,1)S(1)}, bf16[2,128,128]{2,1,0:T(8,128)(2,1)S(1)}, u32[]{:S(2)}, u32[]{:S(2)}) collective-permute-start(bf16[2,128,128]{2,1,0:T(8,128)(2,1)S(1)} %copy-done.7), channel_id=1, source_target_pairs={{0,1},{1,0},{2,3},{3,2},{4,5},{5,4},{6,7},{7,6},{8,9},{9,8},{10,11... | collective-permute-start | bytes 196616 | tf_op jit(solution)/shard_map/ppermute | solution.py:242
  78.4 7.6 %collective-permute-start.5 = (bf16[8,2,2,128,512]{4,3,2,1,0:T(8,128)(2,1)}, bf16[8,2,2,128,512]{4,3,2,1,0:T(8,128)(2,1)}, u32[]{:S(2)}, u32[]{:S(2)}) collective-permute-start(bf16[8,2,2,128,512]{4,3,2,1,0:T(8,128)(2,1)} %bitcast.34), channel_id=1, source_target_pairs={{0,16},{16,0},{32,48},{48,32},{64,80},{80,64},{96,112},{112,96},{1... | collective-permute-start | bytes 12582920 | tf_op jit(solution)/shard_map/ppermute | solution.py:256
  78.5 13.3 %collective-permute-start.4 = (f32[2,8,1024]{2,1,0:T(8,128)S(1)}, f32[2,8,1024]{2,1,0:T(8,128)S(1)}, u32[]{:S(2)}, u32[]{:S(2)}) collective-permute-start(f32[2,8,1024]{2,1,0:T(8,128)S(1)} %copy_bitcast_fusion.near_in), channel_id=1, source_target_pairs={{0,16},{16,0},{32,48},{48,32},{64,80},{80,64},{96,112},{112,96},{1... | collective-permute-start | bytes 196616 | tf_op jit(solution)/shard_map/ppermute | solution.py:252
  95.3 2.9 %collective-permute-start.6 = (f32[8,1024]{1,0:T(8,128)S(1)}, f32[8,1024]{1,0:T(8,128)S(1)}, u32[]{:S(2)}, u32[]{:S(2)}) collective-permute-start(f32[8,1024]{1,0:T(8,128)S(1)} %get-tuple-element.45), channel_id=1, source_target_pairs={{0,32},{16,48},{1,33},{17,49},{2,34},{18,50},{3,35},{19,51},{4,36}... | collective-permute-start | bytes 98312 | tf_op jit(solution)/shard_map/ppermute | solution.py:283
  98.8 0.7 collective-permute-start.7
  100.0 0.7 collective-permute-start.8
  101.2 0.7 collective-permute-start.9
  102.5 0.7 collective-permute-start.10
  103.7 0.7 collective-permute-start.11
  133.6 7.4 %collective-permute-start.14 = (bf16[8,2,2,128,512]{4,3,2,1,0:T(8,128)(2,1)}, bf16[8,2,2,128,512]{4,3,2,1,0:T(8,128)(2,1)S(1)}, u32[]{:S(2)}, u32[]{:S(2)}) collective-permute-start(bf16[8,2,2,128,512]{4,3,2,1,0:T(8,128)(2,1)} %bitcast.32), channel_id=1, source_target_pairs={{0,16},{16,0},{32,48},{48,32},{64,80},{80,64},{96,112},{112,96},{1... | collective-permute-start | bytes 12582920 | tf_op jit(solution)/shard_map/ppermute | solution.py:256
  133.6 11.4 %collective-permute-start.12 = (f32[8,1024]{1,0:T(8,128)S(1)}, f32[8,1024]{1,0:T(8,128)S(1)}, u32[]{:S(2)}, u32[]{:S(2)}) collective-permute-start(f32[8,1024]{1,0:T(8,128)S(1)} %get-tuple-element.57), channel_id=1, source_target_pairs={{192,224},{208,240},{193,225},{209,241},{194,226},{210,242},{195,2... | collective-permute-start | bytes 98312 | tf_op jit(solution)/shard_map/ppermute | solution.py:283
  149.3 0.7 collective-permute-start.15
  150.7 0.7 collective-permute-start.16
  151.9 0.7 collective-permute-start.17
  153.2 0.7 collective-permute-start.18
  154.4 0.7 collective-permute-start.19
  155.7 0.7 collective-permute-start.20
  156.9 54.3 %collective-permute-start.21 = (f32[8,1024]{1,0:T(8,128)S(1)}, f32[8,1024]{1,0:T(8,128)S(1)}, u32[]{:S(2)}, u32[]{:S(2)}) collective-permute-start(f32[8,1024]{1,0:T(8,128)S(1)} %get-tuple-element.78), channel_id=1, source_target_pairs={{32,0},{48,16},{33,1},{49,17},{34,2},{50,18},{35,3},{51,19},{36,4}... | collective-permute-start | bytes 98312 | tf_op jit(solution)/shard_map/ppermute | solution.py:305
  (8 other events, 129.1 us)
Sparse Core Ops, SparseCore 0:
  18.2 60.1 all-gather.4
  80.2 53.4 all-gather.6
where the time goes:
time: 224 us; the launch traced here: 223 us
  waiting for transfers between devices  123 us (55%)
  blocking collectives  25.8 us (12%)
  Pallas kernels  23.6 us (11%)
  starting transfers between devices  19.9 us (9%)
  between operations  13.9 us (6%)
  local copies, waits for them, and re-layouts  9.72 us (4%)
  other arithmetic  6 us (3%)
    ppermute x14, waiting for transfers between devices, on_device(): state = lax.ppermute(sent, 'tm', pairs)  54.6 us
    all_gather x1, waiting for transfers between devices, on_device(): lax.all_gather(jnp.stack([smooth_mats, smooth_other]), 'blk', axis=0)  28.7 us
    all_to_all x2, blocking collectives, all_blocks(): return lax.all_to_all(copies, axis, 0, 0, tiled=True)  25.8 us
    ppermute x2, waiting for transfers between devices, pack(): far = lax.ppermute(value, 'tm', cores)  13.7 us
    ppermute x14, starting transfers between devices, on_device(): state = lax.ppermute(sent, 'tm', pairs)  10.5 us
    pallas_call x8, Pallas kernels, backward(): call(functools.partial(backward_kernel, hop, groups), 'backward', (filt_s...  8.14 us
    unnamed x21, local copies, waits for them, and re-layouts  7.84 us
    ppermute x1, waiting for transfers between devices, on_device(): smooth_other = lax.ppermute(smooth_mats, 'samp', swapped(2))  7.75 us
  transfers between devices with their start and end apart: 24, of which 9 were waited for; matrix products, arithmetic and copies ran while one was open for 4% of the time, Pallas kernels for 5%

commit v1 on v0

--- a/solution.py
+++ b/solution.py
@@ -26,15 +26,17 @@
     return lax.all_to_all(copies, axis, 0, 0, tiled=True)
 
 
-def observation_noise(noise_draw, wend_blocks, block_cols):
-    step_count, sample_count, local_sites = noise_draw.shape
-    block_sites = wend_blocks.shape[1]
-    local_blocks = local_sites // block_sites
-    cycle = lax.axis_size("blk")
-    rim = 2 * block_sites
+def noise_rim(noise_draw, rim=16):
+    cycle, local_sites = lax.axis_size("blk"), noise_draw.shape[2]
     before = lax.ppermute(noise_draw[:, :, local_sites - rim :], "blk", ring(cycle, 1))
     after = lax.ppermute(noise_draw[:, :, :rim], "blk", ring(cycle, -1))
-    widened = jnp.concatenate([before, noise_draw, after], axis=2)
+    return jnp.concatenate([before, noise_draw, after], axis=2)
+
+
+def noise_mixer(wend_blocks, block_cols):
+    block_sites = wend_blocks.shape[1]
+    local_blocks = block_cols.shape[0] // 4
+    cycle = lax.axis_size("blk")
     pair_rows = jnp.arange(local_blocks * 4, dtype=jnp.int32) // 4
     first_block = lax.axis_index("blk") * local_blocks
     offset = (block_cols - first_block - pair_rows + 2) % (local_blocks * cycle)
@@ -44,21 +46,20 @@
     blocks = wend_blocks.reshape(local_blocks, 4, block_sites, block_sites)
     chooser = chooser.reshape(local_blocks, 4, local_blocks + 4)
     mixer = jnp.sum(chooser[:, :, :, None, None] * blocks[:, :, None, :, :], axis=1)
-    mixer = mixer.transpose(1, 3, 0, 2).reshape(local_sites + 2 * rim, local_sites)
-    return jnp.einsum("tsl,lm->tsm", widened, mixer, precision=highest)
+    return mixer.transpose(1, 3, 0, 2).reshape(
+        (local_blocks + 4) * block_sites, local_blocks * block_sites
+    )
 
 
 def split_rows(value):
     high = value.astype(bf16)
-    rest = value - high.astype(f32)
-    middle = rest.astype(bf16)
-    low = (rest - middle.astype(f32)).astype(bf16)
-    return jnp.concatenate([high, middle, low], axis=0)
+    low = (value - high.astype(f32)).astype(bf16)
+    return jnp.concatenate([high, low], axis=0)
 
 
 def joined_rows(value):
-    rows = value.shape[0] // 3
-    return value[:rows] + value[rows : 2 * rows] + value[2 * rows :]
+    rows = value.shape[0] // 2
+    return value[:rows] + value[rows:]
 
 
 def start_copies(shards, out_ref, sems, used, owner, side):
@@ -73,33 +74,12 @@
     return copies
 
 
-def pack_ring_kernel(count, place, near, far, *refs):
-    shards, out_ref, sems = refs[: 2 * count], refs[2 * count], refs[2 * count + 1]
-    blk, samp, core = place[0], place[1], place[2]
-    copies = start_copies(near, out_ref, sems, 0, core, samp)
-    copies += start_copies(far, out_ref, sems, 2, 1 - core, samp)
-    for n, shard in enumerate(shards):
-        whose, k = n // count, n % count
-        steps, rows, width = shard.shape
-        owner = core if whose == 0 else 1 - core
-        at = lax.rem(blk - k + count, count)
-        columns = pl.ds(pl.multiple_of((1 - samp) * width, 128), width)
-        target = out_ref.at[pl.ds(owner * steps, steps), at, :, columns]
-        copy = pltpu.make_async_copy(shard, target, sems.at[4 + n])
-        copy.start()
-        copies.append(copy)
-    for copy in copies:
-        copy.wait()
-
-
-def pack_kernel(place, near, far, out_ref, sems):
+def pack_kernel(far, place, both, *refs):
+    out_ref, sems = refs[-2:]
     samp, core = place[1], place[2]
-    copies = []
-    for whose, shards in enumerate((near, far)):
-        owner = core if whose == 0 else 1 - core
-        for half in range(2):
-            side = samp if half == 0 else 1 - samp
-            copies += start_copies(shards.at[:, half], out_ref, sems, len(copies), owner, side)
+    owner = 1 - core if far else core
+    copies = start_copies(both.at[:, 0], out_ref, sems, 0, owner, samp)
+    copies += start_copies(both.at[:, 1], out_ref, sems, 2, owner, 1 - samp)
     for copy in copies:
         copy.wait()
 
@@ -186,7 +166,6 @@
 
 SMEM = pl.BlockSpec(memory_space=pltpu.SMEM)
 VMEM = pl.BlockSpec(memory_space=pltpu.VMEM)
-ANY = pl.BlockSpec(memory_space=pl.ANY)
 HBM = pl.BlockSpec(memory_space=pltpu.HBM)
 
 
@@ -201,6 +180,10 @@
         compiler_params=pltpu.CompilerParams(vmem_limit_bytes=VMEM_LIMIT),
         name=name,
     )
+
+
+def in_hbm(value):
+    return pltpu.with_memory_space_constraint(value, pltpu.HBM)
 
 
 def in_vmem(value):
@@ -230,10 +213,39 @@
     cores = swapped(times)
     place = jnp.stack([blk, samp, core, group]).astype(jnp.int32)
 
+    mats_shape = jax.ShapeDtypeStruct((4, cycle, trans_mats.shape[1], state_count), bf16)
+
+    def pack(kernel, name, copies, shards, spec, held=None):
+        held = () if held is None else (held,)
+        made = call(
+            kernel,
+            name,
+            mats_shape,
+            [SMEM] + [spec] * len(shards) + [VMEM] * len(held),
+            [pltpu.SemaphoreType.DMA((copies,))],
+            {1 + len(shards): 0} if held else None,
+        )(place, *shards, *held)
+        return in_vmem(made)
+
+    mats_shape = jax.ShapeDtypeStruct((4, cycle, trans_mats.shape[1], state_count), bf16)
+
+    def pack(kernel, name, shards, held=None):
+        held = () if held is None else (held,)
+        made = call(
+            kernel,
+            name,
+            mats_shape,
+            [SMEM, HBM] + [VMEM] * len(held),
+            [pltpu.SemaphoreType.DMA((4,))],
+            {2: 0} if held else None,
+        )(place, in_hbm(shards), *held)
+        return in_vmem(made)
+
     trans_other = lax.ppermute(trans_mats, "samp", swapped(2))
     near = lax.all_gather(jnp.stack([trans_mats, trans_other]), "blk", axis=0)
 
-    obs_noise = observation_noise(noise_draw, wend_blocks, block_cols)
+    widened, mixer = noise_rim(noise_draw), noise_mixer(wend_blocks, block_cols)
+    obs_noise = jnp.einsum("tsl,lm->tsm", widened, mixer, precision=highest)
     first_comp = prior_path.reshape(step_count, sample_count, local_sites, 4)[:, :, :, 0]
     seen_mask = jnp.repeat(obs_mask.astype(f32), block_sites, axis=1)
     residual = seen_mask[:, None, :] * (observed[:, None, :] - first_comp - obs_noise)
@@ -250,15 +262,13 @@
     gathered = gathered.transpose(1, 2, 0, 3).reshape(step_count + 1, sample_count, state_count)
     near_in, start = gathered[:step_count], gathered[step_count]
     far_in = lax.ppermute(near_in, "tm", cores)
-    mats_shape = jax.ShapeDtypeStruct((4, cycle, trans_mats.shape[1], state_count), bf16)
-
-    def pack(value, name):
-        far = lax.ppermute(value, "tm", cores)
-        dmas = [pltpu.SemaphoreType.DMA((8,))]
-        return in_vmem(call(pack_kernel, name, mats_shape, [SMEM, HBM, HBM], dmas)(place, value, far))
+    def pack_all(near, name):
+        far = lax.ppermute(near, "tm", cores)
+        value = pack(functools.partial(pack_kernel, False), name, near)
+        return pack(functools.partial(pack_kernel, True), name, far, value)
 
     near, near_in = lax.optimization_barrier((near, near_in))
-    trans = pack(near, "pack_trans")
+    trans = pack_all(near, "pack_trans")
 
     smooth_mats, _ = lax.optimization_barrier((smooth_mats, all_resid))
     smooth_other = lax.ppermute(smooth_mats, "samp", swapped(2))
@@ -283,7 +293,7 @@
         state = lax.ppermute(sent, "tm", pairs)
         if hop == groups - 1:
             near_smooth, filtered = lax.optimization_barrier((near_smooth, filtered))
-            smooth = pack(near_smooth, "pack_smooth")
+            smooth = pack_all(near_smooth, "pack_smooth")
             filtered, smooth = lax.optimization_barrier((filtered, smooth))
         filtered, sent = forward(hop, state, filtered)
 

time: 224 us -> 217 us (0.969)
  waiting for transfers between devices: 123 us -> 113 us
  Pallas kernels: 23.6 us -> 28.7 us
  local copies, waits for them, and re-layouts: 9.72 us -> 5.91 us
    pallas_call x2 -> x4, Pallas kernels: 5.42 us -> 11.3 us  [pack(): call(kernel, name, mats_shape, [SMEM, HBM] + [VMEM] * len(held), [pltpu.S...]
    ppermute x14, waiting for transfers between devices: 54.6 us -> 48.8 us  [on_device(): state = lax.ppermute(sent, 'tm', pairs)]
    ppermute x4, waiting for transfers between devices: 13.7 us -> 7.87 us  [the longest x2 7.86 us: pack_all(): far = lax.ppermute(near, 'tm', cores)]
    unnamed x21 -> x17, local copies, waits for them, and re-layouts: 7.84 us -> 4.04 us
    all_gather x1, waiting for transfers between devices: 28.7 us -> 32 us  [on_device(): lax.all_gather(jnp.stack([smooth_mats, smooth_other]), 'blk', axis=0)]
  transfers between devices with their start and end apart: 24 -> 24, of which waited for: 9 -> 9; matrix products, arithmetic and copies ran while one was open for 4% -> 5% of each run, Pallas kernels for 5% -> 8%
where the time goes in v1:
time: 217 us; the launch traced here: 216 us
  waiting for transfers between devices  113 us (52%)
  Pallas kernels  28.7 us (13%)
  blocking collectives  25.8 us (12%)
  starting transfers between devices  19.9 us (9%)
  between operations  13.9 us (6%)
  other arithmetic  6.7 us (3%)
  local copies, waits for them, and re-layouts  5.91 us (3%)
    ppermute x14, waiting for transfers between devices, on_device(): state = lax.ppermute(sent, 'tm', pairs)  48.8 us
    all_gather x1, waiting for transfers between devices, on_device(): lax.all_gather(jnp.stack([smooth_mats, smooth_other]), 'blk', axis=0)  32 us
    all_to_all x2, blocking collectives, all_blocks(): return lax.all_to_all(copies, axis, 0, 0, tiled=True)  25.8 us
    pallas_call x4, Pallas kernels, pack(): call(kernel, name, mats_shape, [SMEM, HBM] + [VMEM] * len(held), [pltpu.S...  11.3 us
    ppermute x14, starting transfers between devices, on_device(): state = lax.ppermute(sent, 'tm', pairs)  10.5 us
    ppermute x2, waiting for transfers between devices, pack_all(): far = lax.ppermute(near, 'tm', cores)  7.86 us
    ppermute x1, waiting for transfers between devices, on_device(): smooth_other = lax.ppermute(smooth_mats, 'samp', swapped(2))  7.75 us
    ppermute x1, waiting for transfers between devices, on_device(): trans_other = lax.ppermute(trans_mats, 'samp', swapped(2))  7.69 us
  transfers between devices with their start and end apart: 24, of which 9 were waited for; matrix products, arithmetic and copies ran while one was open for 5% of the time, Pallas kernels for 8%

profile of v1, /device:TPU:16, one launch (start us, length us, event | category | flops | bytes accessed | tf_op | source)
XLA Modules:
  0.0 216.3 jit_solution(1239961404423142116)
XLA Ops:
  6.5 2.1 collective-permute-start.3
  8.6 7.7 %collective-permute-done.3 = bf16[2,128,512]{2,1,0:T(8,128)(2,1)S(1)} collective-permute-done((bf16[2,128,512]{2,1,0:T(8,128)(2,1)}, bf16[2,128,512]{2,1,0:T(8,128)(2,1)S(1)}, u32[]{:S(2)}, u32[]{:S(2)}) %collective-permute-start.3) | collective-permute-done | bytes 262176 | tf_op jit(solution)/shard_map/ppermute | solution.py:244
  16.3 1.8 pad_maximum_fusion
  19.0 1.9 collective-permute-start
  20.9 4.0 %collective-permute-start.1 = (f32[2,8,16]{2,1,0:T(8,128)S(1)}, f32[2,8,16]{2,1,0:T(8,128)S(1)}, u32[]{:S(2)}, u32[]{:S(2)}) collective-permute-start(f32[2,8,16]{2,1,0:T(8,128)S(1)} %get-tuple-element.82), channel_id=1, source_target_pairs={{0,14},{2,0},{4,2},{6,4},{8,6},{10,8},{12,10},{14,12},{1,15},{3,1}... | collective-permute-start | bytes 3080 | tf_op jit(solution)/shard_map/ppermute | solution.py:32
  29.7 13.6 %all_to_all.10 = f32[8,1,512]{2,1,0:T(1,128)S(1)} all-to-all(f32[8,1,512]{2,1,0:T(1,128)S(1)} %reshape.39), channel_id=1, replica_groups=mesh['tm'=16,'blk'=8,'samp'=2] {'blk'}, dimensions={0} | all-to-all | bytes 32768 | tf_op jit(solution)/shard_map/all_to_all | solution.py:26
  45.2 7.8 %collective-permute-done.13 = bf16[2,128,512]{2,1,0:T(8,128)(2,1)S(1)} collective-permute-done((bf16[2,128,512]{2,1,0:T(8,128)(2,1)}, bf16[2,128,512]{2,1,0:T(8,128)(2,1)S(1)}, u32[]{:S(2)}, u32[]{:S(2)}) %collective-permute-start.13) | collective-permute-done | bytes 262176 | tf_op jit(solution)/shard_map/ppermute | solution.py:274
  52.9 1.8 pad_maximum_fusion.1
  55.2 5.6 %collective-permute-done.2 = bf16[2,128,128]{2,1,0:T(8,128)(2,1)S(1)} collective-permute-done((bf16[2,128,128]{2,1,0:T(8,128)(2,1)}, bf16[2,128,128]{2,1,0:T(8,128)(2,1)S(1)}, u32[]{:S(2)}, u32[]{:S(2)}) %collective-permute-start.2) | collective-permute-done | bytes 65568 | tf_op jit(solution)/shard_map/ppermute | solution.py:254
  62.7 12.1 %all_to_all.11 = f32[8,3,8,128]{3,2,1,0:T(8,128)S(1)} all-to-all(f32[8,3,8,128]{3,2,1,0:T(8,128)S(1)} %broadcast_in_dim.11), channel_id=1, replica_groups=mesh['tm'=16,'blk'=8,'samp'=2] {'blk'}, dimensions={0} | all-to-all | bytes 196608 | tf_op jit(solution)/shard_map/all_to_all | solution.py:26
  74.8 3.6 %all-gather.5.cloned.1.call-done = bf16[16,2,128,512]{3,2,1,0:T(8,128)(2,1)} async-done(((bf16[2,2,128,512]{3,2,1,0:T(8,128)(2,1)}), bf16[16,2,128,512]{3,2,1,0:T(8,128)(2,1)}) %all-gather.5.cloned.1.call-update) | async-done | bytes 4194320 | tf_op jit(solution)/shard_map/all_gather | solution.py:245
  79.0 2.8 %pack_trans.2.refs_0_ = bf16[4,8,128,1024]{3,2,1,0:T(8,128)(2,1)S(1)} custom-call(s32[4]{0:T(128)S(1)} %pad_add_fusion.place, bf16[8,2,2,128,512]{4,3,2,1,0:T(8,128)(2,1)} %bitcast.37), custom_call_target="tpu_custom_call" | custom-call | tf_op jit(solution)/shard_map/pack_trans/pallas_call | solution.py:234
  81.8 4.2 %collective-permute-done.5.both = bf16[8,2,2,128,512]{4,3,2,1,0:T(8,128)(2,1)} collective-permute-done((bf16[8,2,2,128,512]{4,3,2,1,0:T(8,128)(2,1)}, bf16[8,2,2,128,512]{4,3,2,1,0:T(8,128)(2,1)}, u32[]{:S(2)}, u32[]{:S(2)}) %collective-permute-start.5) | collective-permute-done | bytes 4194336 | tf_op jit(solution)/shard_map/ppermute | solution.py:266
  86.0 2.8 %pack_trans.3.mats = bf16[4,8,128,1024]{3,2,1,0:T(8,128)(2,1)S(1)} custom-call(s32[4]{0:T(128)S(1)} %pad_add_fusion.place, bf16[8,2,2,128,512]{4,3,2,1,0:T(8,128)(2,1)} %collective-permute-done.5.both, bf16[4,8,128,1024]{3,2,1,0:T(8,128)(2,1)S(1)} %pack_trans.2.refs_0_), custom_call_target="tpu_custom_call", output_to_operand_aliasing={{}: (2, {})} | custom-call | tf_op jit(solution)/shard_map/pack_trans/pallas_call | solution.py:234
  88.8 3.2 %forward.8 = (f32[4,8,1024]{2,1,0:T(8,128)S(1)}, f32[8,1024]{1,0:T(8,128)S(1)}) custom-call(s32[4]{0:T(128)S(1)} %pad_add_fusion.place, f32[8,1024]{1,0:T(8,128)S(1)} %slice_bitcast_fusion.state_ref, f32[2,8,1024]{2,1,0:T(8,128)S(1)} %copy_bitcast_fusion.near_in, f32[2,8,1024]{2,1,0:T(8,128)S(1)} %collective-permute-done.4.far_in, ...), custom_call_target="tpu_custom_call" | custom-call | tf_op jit(solution)/shard_map/forward/pallas_call | solution.py:281
  93.3 1.6 collective-permute-done.6.state_ref
  101.6 32.0 %all-gather.7.cloned.1.call-done = bf16[16,2,128,512]{3,2,1,0:T(8,128)(2,1)} async-done(((bf16[2,2,128,512]{3,2,1,0:T(8,128)(2,1)}), bf16[16,2,128,512]{3,2,1,0:T(8,128)(2,1)}) %all-gather.7.cloned.1.call-update) | async-done | bytes 4194320 | tf_op jit(solution)/shard_map/all_gather | solution.py:275
  134.3 3.0 %pack_smooth.2.refs_0_ = bf16[4,8,128,1024]{3,2,1,0:T(8,128)(2,1)S(1)} custom-call(s32[4]{0:T(128)S(1)} %pad_add_fusion.place, bf16[8,2,2,128,512]{4,3,2,1,0:T(8,128)(2,1)} %bitcast.35), custom_call_target="tpu_custom_call" | custom-call | tf_op jit(solution)/shard_map/pack_smooth/pallas_call | solution.py:234
  137.4 3.6 %collective-permute-done.14.both = bf16[8,2,2,128,512]{4,3,2,1,0:T(8,128)(2,1)S(1)} collective-permute-done((bf16[8,2,2,128,512]{4,3,2,1,0:T(8,128)(2,1)}, bf16[8,2,2,128,512]{4,3,2,1,0:T(8,128)(2,1)S(1)}, u32[]{:S(2)}, u32[]{:S(2)}) %collective-permute-start.14) | collective-permute-done | bytes 4194336 | tf_op jit(solution)/shard_map/ppermute | solution.py:266
  141.0 2.0 copy-done.3
  143.1 2.8 %pack_smooth.3.mats = bf16[4,8,128,1024]{3,2,1,0:T(8,128)(2,1)S(1)} custom-call(s32[4]{0:T(128)S(1)} %pad_add_fusion.place, bf16[8,2,2,128,512]{4,3,2,1,0:T(8,128)(2,1)} %copy-done.3, bf16[4,8,128,1024]{3,2,1,0:T(8,128)(2,1)S(1)} %pack_smooth.2.refs_0_), custom_call_target="tpu_custom_call", output_to_operand_aliasing={{}: (2, {})} | custom-call | tf_op jit(solution)/shard_map/pack_smooth/pallas_call | solution.py:234
  146.5 1.5 predict.1.pred_ref
  157.4 47.1 %collective-permute-done.21.state_ref = f32[8,1024]{1,0:T(8,128)S(1)} collective-permute-done((f32[8,1024]{1,0:T(8,128)S(1)}, f32[8,1024]{1,0:T(8,128)S(1)}, u32[]{:S(2)}, u32[]{:S(2)}) %collective-permute-start.21) | collective-permute-done | bytes 32800 | tf_op jit(solution)/shard_map/ppermute | solution.py:315
  204.5 3.8 %backward.15 = (f32[4,8,1024]{2,1,0:T(8,128)S(1)}, f32[8,1024]{1,0:T(8,128)}) custom-call(s32[4]{0:T(128)S(1)} %pad_add_fusion.place, f32[8,1024]{1,0:T(8,128)S(1)} %collective-permute-done.21.state_ref, f32[4,8,1024]{2,1,0:T(8,128)S(1)} %get-tuple-element.64.filt_ref, f32[4,8,1024]{2,1,0:T(8,128)S(1)} %predict.1.pred_ref, ...), custom_call_target="tpu_custom_call", output_to_operand_aliasing={{0}: (5, {})} | custom-call | tf_op jit(solution)/shard_map/backward/pallas_call | solution.py:303
  (93 shorter events, 29.9 us)
Async XLA Ops:
  6.5 71.9 %all-gather.5.cloned.1.call-start = ((), (), s32[]{:S(2)}) async-start(), calls=%async_computation.2 | async-start | bytes 4718592 | tf_op jit(solution)/shard_map/all_gather | solution.py:245
  6.5 9.8 %collective-permute-start.3 = (bf16[2,128,512]{2,1,0:T(8,128)(2,1)}, bf16[2,128,512]{2,1,0:T(8,128)(2,1)S(1)}, u32[]{:S(2)}, u32[]{:S(2)}) collective-permute-start(bf16[2,128,512]{2,1,0:T(8,128)(2,1)} %param.18), channel_id=1, source_target_pairs={{0,1},{1,0},{2,3},{3,2},{4,5},{5,4},{6,7},{7,6},{8,9},{9,8},{10,11... | collective-permute-start | bytes 786440 | tf_op jit(solution)/shard_map/ppermute | solution.py:244
  18.1 115.5 %all-gather.7.cloned.1.call-start = ((), (), s32[]{:S(2)}) async-start(), calls=%async_computation.3 | async-start | bytes 4718592 | tf_op jit(solution)/shard_map/all_gather | solution.py:275
  19.0 9.7 %collective-permute-start = (f32[2,8,16]{2,1,0:T(8,128)S(1)}, f32[2,8,16]{2,1,0:T(8,128)S(1)}, u32[]{:S(2)}, u32[]{:S(2)}) collective-permute-start(f32[2,8,16]{2,1,0:T(8,128)S(1)} %get-tuple-element.81), channel_id=1, source_target_pairs={{0,2},{2,4},{4,6},{6,8},{8,10},{10,12},{12,14},{14,0},{1,3},{3,5},... | collective-permute-start | bytes 3080 | tf_op jit(solution)/shard_map/ppermute | solution.py:31
  20.9 7.8 %collective-permute-start.1 = (f32[2,8,16]{2,1,0:T(8,128)S(1)}, f32[2,8,16]{2,1,0:T(8,128)S(1)}, u32[]{:S(2)}, u32[]{:S(2)}) collective-permute-start(f32[2,8,16]{2,1,0:T(8,128)S(1)} %get-tuple-element.82), channel_id=1, source_target_pairs={{0,14},{2,0},{4,2},{6,4},{8,6},{10,8},{12,10},{14,12},{1,15},{3,1}... | collective-permute-start | bytes 3080 | tf_op jit(solution)/shard_map/ppermute | solution.py:32
  44.8 8.2 %collective-permute-start.13 = (bf16[2,128,512]{2,1,0:T(8,128)(2,1)}, bf16[2,128,512]{2,1,0:T(8,128)(2,1)S(1)}, u32[]{:S(2)}, u32[]{:S(2)}) collective-permute-start(bf16[2,128,512]{2,1,0:T(8,128)(2,1)} %param.20), channel_id=1, source_target_pairs={{0,1},{1,0},{2,3},{3,2},{4,5},{5,4},{6,7},{7,6},{8,9},{9,8},{10,11... | collective-permute-start | bytes 786440 | tf_op jit(solution)/shard_map/ppermute | solution.py:274
  54.8 6.1 %collective-permute-start.2 = (bf16[2,128,128]{2,1,0:T(8,128)(2,1)}, bf16[2,128,128]{2,1,0:T(8,128)(2,1)S(1)}, u32[]{:S(2)}, u32[]{:S(2)}) collective-permute-start(bf16[2,128,128]{2,1,0:T(8,128)(2,1)} %param.19), channel_id=1, source_target_pairs={{0,1},{1,0},{2,3},{3,2},{4,5},{5,4},{6,7},{7,6},{8,9},{9,8},{10,11... | collective-permute-start | bytes 196616 | tf_op jit(solution)/shard_map/ppermute | solution.py:254
  78.4 7.6 %collective-permute-start.5 = (bf16[8,2,2,128,512]{4,3,2,1,0:T(8,128)(2,1)}, bf16[8,2,2,128,512]{4,3,2,1,0:T(8,128)(2,1)}, u32[]{:S(2)}, u32[]{:S(2)}) collective-permute-start(bf16[8,2,2,128,512]{4,3,2,1,0:T(8,128)(2,1)} %bitcast.36), channel_id=1, source_target_pairs={{0,16},{16,0},{32,48},{48,32},{64,80},{80,64},{96,112},{112,96},{1... | collective-permute-start | bytes 12582920 | tf_op jit(solution)/shard_map/ppermute | solution.py:266
  78.5 10.3 %collective-permute-start.4 = (f32[2,8,1024]{2,1,0:T(8,128)S(1)}, f32[2,8,1024]{2,1,0:T(8,128)S(1)}, u32[]{:S(2)}, u32[]{:S(2)}) collective-permute-start(f32[2,8,1024]{2,1,0:T(8,128)S(1)} %copy_bitcast_fusion.near_in), channel_id=1, source_target_pairs={{0,16},{16,0},{32,48},{48,32},{64,80},{80,64},{96,112},{112,96},{1... | collective-permute-start | bytes 196616 | tf_op jit(solution)/shard_map/ppermute | solution.py:264
  92.0 2.9 %collective-permute-start.6 = (f32[8,1024]{1,0:T(8,128)S(1)}, f32[8,1024]{1,0:T(8,128)S(1)}, u32[]{:S(2)}, u32[]{:S(2)}) collective-permute-start(f32[8,1024]{1,0:T(8,128)S(1)} %get-tuple-element.45), channel_id=1, source_target_pairs={{0,32},{16,48},{1,33},{17,49},{2,34},{18,50},{3,35},{19,51},{4,36}... | collective-permute-start | bytes 98312 | tf_op jit(solution)/shard_map/ppermute | solution.py:293
  95.4 0.7 collective-permute-start.7
  96.6 0.7 collective-permute-start.8
  97.9 0.7 collective-permute-start.9
  99.1 0.7 collective-permute-start.10
  100.4 0.7 collective-permute-start.11
  133.6 7.4 %collective-permute-start.14 = (bf16[8,2,2,128,512]{4,3,2,1,0:T(8,128)(2,1)}, bf16[8,2,2,128,512]{4,3,2,1,0:T(8,128)(2,1)S(1)}, u32[]{:S(2)}, u32[]{:S(2)}) collective-permute-start(bf16[8,2,2,128,512]{4,3,2,1,0:T(8,128)(2,1)} %bitcast.34), channel_id=1, source_target_pairs={{0,16},{16,0},{32,48},{48,32},{64,80},{80,64},{96,112},{112,96},{1... | collective-permute-start | bytes 12582920 | tf_op jit(solution)/shard_map/ppermute | solution.py:266
  133.6 12.2 %collective-permute-start.12 = (f32[8,1024]{1,0:T(8,128)S(1)}, f32[8,1024]{1,0:T(8,128)S(1)}, u32[]{:S(2)}, u32[]{:S(2)}) collective-permute-start(f32[8,1024]{1,0:T(8,128)S(1)} %get-tuple-element.57), channel_id=1, source_target_pairs={{192,224},{208,240},{193,225},{209,241},{194,226},{210,242},{195,2... | collective-permute-start | bytes 98312 | tf_op jit(solution)/shard_map/ppermute | solution.py:293
  148.6 0.7 collective-permute-start.15
  149.9 0.7 collective-permute-start.16
  151.1 0.7 collective-permute-start.17
  152.3 0.7 collective-permute-start.18
  153.6 0.7 collective-permute-start.19
  154.8 0.7 collective-permute-start.20
  156.1 48.4 %collective-permute-start.21 = (f32[8,1024]{1,0:T(8,128)S(1)}, f32[8,1024]{1,0:T(8,128)S(1)}, u32[]{:S(2)}, u32[]{:S(2)}) collective-permute-start(f32[8,1024]{1,0:T(8,128)S(1)} %get-tuple-element.78), channel_id=1, source_target_pairs={{32,0},{48,16},{33,1},{49,17},{34,2},{50,18},{35,3},{51,19},{36,4}... | collective-permute-start | bytes 98312 | tf_op jit(solution)/shard_map/ppermute | solution.py:315
  (6 other events, 87.9 us)
Sparse Core Ops, SparseCore 0:
  18.2 60.1 all-gather.4
  80.2 53.4 all-gather.6

commit v2 on v1

v2 whole, which is shorter than its diff:
```python
import functools
import jax
import jax.numpy as jnp
from jax import lax
from jax.experimental import pallas as pl
from jax.experimental.pallas import tpu as pltpu
from jax.sharding import PartitionSpec as P

highest = lax.Precision.HIGHEST
bf16, f32 = jnp.bfloat16, jnp.float32
ROWS_BY_ROWS = (((1,), (1,)), ((), ()))
VMEM_LIMIT = 2 * 1024 * 1024


def ring(count, step):
    return [(i, (i + step) % count) for i in range(count)]


def swapped(count):
    return [(i, i ^ 1) for i in range(count)]


def all_blocks(value, axis):
    count = lax.axis_size(axis)
    copies = jnp.broadcast_to(value[None], (count,) + value.shape)
    return lax.all_to_all(copies, axis, 0, 0, tiled=True)


def noise_rim(noise_draw, rim=16):
    cycle, local_sites = lax.axis_size("blk"), noise_draw.shape[2]
    before = lax.ppermute(noise_draw[:, :, local_sites - rim :], "blk", ring(cycle, 1))
    after = lax.ppermute(noise_draw[:, :, :rim], "blk", ring(cycle, -1))
    return jnp.concatenate([before, noise_draw, after], axis=2)


def noise_mixer(wend_blocks, block_cols):
    block_sites = wend_blocks.shape[1]
    local_blocks = block_cols.shape[0] // 4
    cycle = lax.axis_size("blk")
    pair_rows = jnp.arange(local_blocks * 4, dtype=jnp.int32) // 4
    first_block = lax.axis_index("blk") * local_blocks
    offset = (block_cols - first_block - pair_rows + 2) % (local_blocks * cycle)
    chooser = (
        (pair_rows + offset)[:, None] == jnp.arange(local_blocks + 4, dtype=jnp.int32)[None, :]
    ).astype(f32)
    blocks = wend_blocks.reshape(local_blocks, 4, block_sites, block_sites)
    chooser = chooser.reshape(local_blocks, 4, local_blocks + 4)
    mixer = jnp.sum(chooser[:, :, :, None, None] * blocks[:, :, None, :, :], axis=1)
    return mixer.transpose(1, 3, 0, 2).reshape(
        (local_blocks + 4) * block_sites, local_blocks * block_sites
    )


def split_rows(value):
    high = value.astype(bf16)
    low = (value - high.astype(f32)).astype(bf16)
    return jnp.concatenate([high, low], axis=0)


def joined_rows(value):
    rows = value.shape[0] // 2
    return value[:rows] + value[rows:]


def pack_kernel(parts, rows_ref, out_ref, sems):
    cores, count, steps = rows_ref.shape[:3]
    copies = []
    for core in range(cores):
        for step in range(steps):
            for part in range(parts):
                blocks = pl.ds(part * (count // parts), count // parts)
                copy = pltpu.make_async_copy(
                    rows_ref.at[core, blocks, step],
                    out_ref.at[core * steps + step, blocks],
                    sems.at[len(copies)],
                )
                copy.start()
                copies.append(copy)
    for copy in copies:
        copy.wait()


def apply_rows(mats, turn, value, store):
    count, rows, _ = mats.shape[1:]
    terms = split_rows(value)
    for k in range(0, count, 2):
        block = jnp.concatenate([mats[turn, k], mats[turn, k + 1]], axis=0)
        part = lax.dot_general(terms, block, ROWS_BY_ROWS, preferred_element_type=f32)
        store(slice(k * rows, (k + 2) * rows), joined_rows(part))


def forward_kernel(hop, state_ref, near_in, far_in, mats, *refs):
    filt_ref, sent_ref = refs[-2:]

    @pl.when(lax.axis_index("chip") == hop)
    def _():
        sent_ref[...] = state_ref[...]

        def step(turn, carry):
            is_near = turn // 2 == lax.axis_index("core")

            def store(columns, part):
                at = lax.rem(turn, 2)
                added = jnp.where(is_near, near_in[at, :, columns], far_in[at, :, columns])
                filt_ref[turn, :, columns] = part + added

            apply_rows(mats, turn, sent_ref[...], store)
            sent_ref[...] = filt_ref[turn]
            return carry

        lax.fori_loop(0, 4, step, 0)


def backward_kernel(hop, hops, state_ref, filt_ref, pred_ref, mats, *refs):
    target_ref, sent_ref = refs[-2:]

    @pl.when(lax.axis_index("chip") == hop)
    def _():
        sent_ref[...] = state_ref[...]

        def step(i, carry):
            turn = 3 - i
            change = sent_ref[...] - pred_ref[turn]
            if hop == hops - 1:
                change = jnp.where(turn == 3, 0.0, change)

            def store(columns, part):
                target_ref[turn, :, columns] = filt_ref[turn, :, columns] + part

            apply_rows(mats, turn, change, store)
            sent_ref[...] = target_ref[turn]
            return carry

        lax.fori_loop(0, 4, step, 0)


def finish_kernel(prior_ref, smooth_ref, out_ref):
    width = out_ref.shape[2]
    columns = pl.ds(pl.multiple_of(lax.axis_index("blk") * width, 128), width)
    for step in range(2):
        out_ref[step] = prior_ref[step] + smooth_ref[lax.axis_index("core") * 2 + step, :, columns]


def kron_kernel(site_ref, out_ref):
    row = lax.broadcasted_iota(jnp.int32, out_ref.shape, 0)
    column = lax.broadcasted_iota(jnp.int32, out_ref.shape, 1)
    same_site = row // 4 == column // 4
    kron = jnp.zeros(out_ref.shape, f32)
    for i in range(4):
        for j in range(4):
            here = same_site & (row % 4 == i) & (column % 4 == j)
            kron = jnp.where(here, site_ref[i, j], kron)
    out_ref[...] = kron


def predict_kernel(kron_ref, filt_ref, out_ref):
    steps, samples, states = filt_ref.shape
    width = kron_ref.shape[0]
    for k in range(0, states, width):
        rows = filt_ref[:, :, k : k + width].reshape(steps * samples, width)
        moved = lax.dot_general(
            rows, kron_ref[...], ROWS_BY_ROWS, precision=highest, preferred_element_type=f32
        )
        out_ref[:, :, k : k + width] = moved.reshape(steps, samples, width)


SMEM = pl.BlockSpec(memory_space=pltpu.SMEM)
VMEM = pl.BlockSpec(memory_space=pltpu.VMEM)
HBM = pl.BlockSpec(memory_space=pltpu.HBM)


def call(kernel, name, shapes, specs, scratch=(), aliases=None):
    return pl.pallas_call(
        kernel,
        out_shape=shapes,
        in_specs=specs,
        out_specs=jax.tree.map(lambda _: VMEM, shapes),
        scratch_shapes=list(scratch),
        input_output_aliases=aliases or {},
        compiler_params=pltpu.CompilerParams(vmem_limit_bytes=VMEM_LIMIT),
        name=name,
    )


def in_hbm(value):
    return pltpu.with_memory_space_constraint(value, pltpu.HBM)


def in_vmem(value):
    return pltpu.with_memory_space_constraint(value, pltpu.VMEM)


def on_device(
    prior_path,
    observed,
    obs_mask,
    noise_draw,
    wend_blocks,
    block_cols,
    start_mean,
    trans_mats,
    gain_mats,
    smooth_mats,
    site_trans,
):
    cycle, groups = lax.axis_size("blk"), lax.axis_size("chip")
    step_count, sample_count, local_sites = noise_draw.shape
    block_sites = wend_blocks.shape[1]
    state_count = trans_mats.shape[1] * cycle

    mats_shape = jax.ShapeDtypeStruct((4, cycle, trans_mats.shape[1], state_count), bf16)

    def all_rows(mats):
        whole = lax.all_gather(mats, "samp", axis=2, tiled=True)
        rows = lax.all_gather(whole, ("core", "blk"), axis=0)
        return rows.reshape((2, cycle) + rows.shape[1:])

    def pack(rows, name):
        parts = 4
        made = call(
            functools.partial(pack_kernel, parts),
            name,
            mats_shape,
            [HBM],
            [pltpu.SemaphoreType.DMA((4 * parts,))],
        )(in_hbm(rows))
        return in_vmem(made)

    trans_rows = all_rows(trans_mats)

    widened, mixer = noise_rim(noise_draw), noise_mixer(wend_blocks, block_cols)
    obs_noise = jnp.einsum("tsl,lm->tsm", widened, mixer, precision=highest)
    first_comp = prior_path.reshape(step_count, sample_count, local_sites, 4)[:, :, :, 0]
    seen_mask = jnp.repeat(obs_mask.astype(f32), block_sites, axis=1)
    residual = seen_mask[:, None, :] * (observed[:, None, :] - first_comp - obs_noise)
    all_resid = all_blocks(residual, "blk").transpose(1, 2, 0, 3)
    all_resid = all_resid.reshape(step_count, sample_count, local_sites * cycle)
    gain = lax.all_gather(gain_mats, "samp", axis=2, tiled=True)
    inputs = jnp.einsum("tij,tsj->tsi", gain, all_resid, precision=highest)
    gathered = all_blocks(jnp.concatenate([inputs, start_mean[None]], axis=0), "blk")
    gathered = gathered.transpose(1, 2, 0, 3).reshape(step_count + 1, sample_count, state_count)
    near_in, start = gathered[:step_count], gathered[step_count]
    far_in = lax.ppermute(near_in, "core", swapped(2))
    trans_rows, near_in = lax.optimization_barrier((trans_rows, near_in))
    trans = pack(trans_rows, "pack_trans")

    smooth_mats, _ = lax.optimization_barrier((smooth_mats, all_resid))
    smooth_rows = all_rows(smooth_mats)

    filt_shape = jax.ShapeDtypeStruct((4, sample_count, state_count), f32)
    state_shape = jax.ShapeDtypeStruct((sample_count, state_count), f32)

    def forward(hop, state, *filtered):
        return call(
            functools.partial(forward_kernel, hop),
            "forward",
            (filt_shape, state_shape),
            [VMEM] * (4 + len(filtered)),
            (),
            {4: 0} if filtered else None,
        )(state, near_in, far_in, trans, *filtered)

    kron_shape = jax.ShapeDtypeStruct((128, 128), f32)
    kron = in_vmem(call(kron_kernel, "kron", kron_shape, [SMEM])(site_trans))
    kron, start = lax.optimization_barrier((kron, start))
    filtered, sent = forward(0, start)
    for hop in range(1, groups):
        state = lax.ppermute(sent, "chip", [(hop - 1, hop)])
        if hop == groups - 1:
            smooth_rows, filtered = lax.optimization_barrier((smooth_rows, filtered))
            smooth = pack(smooth_rows, "pack_smooth")
            filtered, smooth = lax.optimization_barrier((filtered, smooth))
        filtered, sent = forward(hop, state, filtered)

    predicted = call(predict_kernel, "predict", filt_shape, [VMEM, VMEM])(kron, filtered)

    def backward(hop, state, *smoothed):
        return call(
            functools.partial(backward_kernel, hop, groups),
            "backward",
            (filt_shape, state_shape),
            [VMEM] * (4 + len(smoothed)),
            (),
            {4: 0} if smoothed else None,
        )(state, filtered, predicted, smooth, *smoothed)

    smoothed, sent = backward(groups - 1, sent)
    for hop in range(groups - 2, -1, -1):
        state = lax.ppermute(sent, "chip", [(hop + 1, hop)])
        smoothed, sent = backward(hop, state, smoothed)
    out_shape = jax.ShapeDtypeStruct(prior_path.shape, f32)
    return call(finish_kernel, "finish", out_shape, [VMEM, VMEM])(prior_path, smoothed)


def solution(mesh):
    times, cycle, samples = mesh.devices.shape
    by_chip = jax.sharding.Mesh(
        mesh.devices.reshape(times // 2, 2, cycle, samples), ("chip", "core", "blk", "samp")
    )
    time = ("chip", "core")
    placed = (
        P(time, "samp", "blk"),
        P(time, "blk"),
        P(time, "blk"),
        P(time, "samp", "blk"),
        P("blk", None, None),
        P("blk"),
        P("samp", "blk"),
        P(time, "blk", "samp"),
        P(time, "blk", "samp"),
        P(time, "blk", "samp"),
        P(),
    )
    return jax.shard_map(
        on_device, mesh=by_chip, in_specs=placed, out_specs=P(time, "samp", "blk"), check_vma=False
    )
```

time: 217 us -> 206 us (0.949)
  blocking collectives: 25.8 us -> 39.8 us
  Pallas kernels: 28.7 us -> 15.4 us
  waiting for transfers between devices: 113 us -> 105 us
  other arithmetic: 6.7 us -> 3.02 us
    ppermute x20 -> x15, waiting for transfers between devices: 77.7 us -> 48.8 us  [the longest x7 47.2 us: on_device(): state = lax.ppermute(sent, 'chip', [(hop + 1, hop)])]
    all_gather x0 -> x3, blocking collectives: none -> 26.1 us  [the longest x2 19.5 us: all_rows(): whole = lax.all_gather(mats, 'samp', axis=2, tiled=True)]
    all_to_all x2 -> x1, blocking collectives: 25.8 us -> 13.6 us  [all_blocks(): return lax.all_to_all(copies, axis, 0, 0, tiled=True)]
    all_gather x2, waiting for transfers between devices: 35.6 us -> 47.6 us  [all_rows(): rows = lax.all_gather(whole, ('core', 'blk'), axis=0)]
    all_to_all x0 -> x1, waiting for transfers between devices: none -> 8.32 us  [all_blocks(): return lax.all_to_all(copies, axis, 0, 0, tiled=True)]
    pallas_call x6 -> x5, Pallas kernels: 14 us -> 9.33 us  [the longest x2 7.17 us: pack(): call(functools.partial(pack_kernel, parts), name, mats_shape, [HBM], [plt...]
    pallas_call x8, Pallas kernels: 7.68 us -> 3.36 us  [backward(): call(functools.partial(backward_kernel, hop, groups), 'backward', (filt_s...]
    pallas_call x8, Pallas kernels: 7.04 us -> 2.74 us  [forward(): call(functools.partial(forward_kernel, hop), 'forward', (filt_shape, stat...]
  transfers between devices with their start and end apart: 24 -> 20, of which waited for: 9 -> 5; matrix products, arithmetic and copies ran while one was open for 5% -> 4% of each run, Pallas kernels for 8% -> 5%
where the time goes in v2:
time: 206 us; the launch traced here: 205 us
  waiting for transfers between devices  105 us (51%)
  blocking collectives  39.8 us (19%)
  starting transfers between devices  19.8 us (10%)
  Pallas kernels  15.4 us (7%)
  between operations  13.9 us (7%)
  local copies, waits for them, and re-layouts  7.3 us (4%)
  other arithmetic  3.02 us (1%)
    all_gather x2, waiting for transfers between devices, all_rows(): rows = lax.all_gather(whole, ('core', 'blk'), axis=0)  47.6 us
    ppermute x7, waiting for transfers between devices, on_device(): state = lax.ppermute(sent, 'chip', [(hop + 1, hop)])  47.2 us
    all_gather x2, blocking collectives, all_rows(): whole = lax.all_gather(mats, 'samp', axis=2, tiled=True)  19.5 us
    all_to_all x1, blocking collectives, all_blocks(): return lax.all_to_all(copies, axis, 0, 0, tiled=True)  13.6 us
    all_to_all x1, waiting for transfers between devices, all_blocks(): return lax.all_to_all(copies, axis, 0, 0, tiled=True)  8.32 us
    pallas_call x2, Pallas kernels, pack(): call(functools.partial(pack_kernel, parts), name, mats_shape, [HBM], [plt...  7.17 us
    all_gather x1, blocking collectives, on_device(): gain = lax.all_gather(gain_mats, 'samp', axis=2, tiled=True)  6.68 us
    ppermute x7, starting transfers between devices, on_device(): state = lax.ppermute(sent, 'chip', [(hop + 1, hop)])  5.29 us
  transfers between devices with their start and end apart: 20, of which 5 were waited for; matrix products, arithmetic and copies ran while one was open for 4% of the time, Pallas kernels for 5%

profile of v2, /device:TPU:16, one launch (start us, length us, event | category | flops | bytes accessed | tf_op | source)
XLA Modules:
  0.0 205.1 jit_solution(6782447957762731774)
XLA Ops:
  6.5 10.5 %all_gather.22 = bf16[2,128,1024]{2,1,0:T(8,128)(2,1)} all-gather(bf16[2,128,512]{2,1,0:T(8,128)(2,1)} %param.18), channel_id=1, replica_groups=mesh['chip'=8,'core'=2,'blk'=8,'samp'=2] {'samp'}, dimensions={2}, use_global_device_ids=true | all-gather | bytes 786432 | tf_op jit(solution)/shard_map/all_gather | solution.py:214
  17.1 0.8 fusion.10
  18.0 1.9 collective-permute-start
  19.9 4.0 %collective-permute-start.1 = (f32[2,8,16]{2,1,0:T(8,128)S(1)}, f32[2,8,16]{2,1,0:T(8,128)S(1)}, u32[]{:S(2)}, u32[]{:S(2)}) collective-permute-start(f32[2,8,16]{2,1,0:T(8,128)S(1)} %get-tuple-element.86), channel_id=1, source_target_pairs={{0,14},{2,0},{4,2},{6,4},{8,6},{10,8},{12,10},{14,12},{1,15},{3,1}... | collective-permute-start | bytes 3080 | tf_op jit(solution)/shard_map/ppermute | solution.py:32
  24.6 0.8 copy.42
  26.7 0.8 copy.40
  27.7 0.9 fusion
  28.7 13.6 %all_to_all.10 = f32[8,1,512]{2,1,0:T(1,128)S(1)} all-to-all(f32[8,1,512]{2,1,0:T(1,128)S(1)} %reshape.49), channel_id=1, replica_groups=mesh['chip'=8,'core'=2,'blk'=8,'samp'=2] {'blk'}, dimensions={0} | all-to-all | bytes 32768 | tf_op jit(solution)/shard_map/all_to_all | solution.py:26
  43.7 8.9 %all_gather.25 = bf16[2,128,1024]{2,1,0:T(8,128)(2,1)} all-gather(bf16[2,128,512]{2,1,0:T(8,128)(2,1)} %param.20), channel_id=1, replica_groups=mesh['chip'=8,'core'=2,'blk'=8,'samp'=2] {'samp'}, dimensions={2}, use_global_device_ids=true | all-gather | bytes 786432 | tf_op jit(solution)/shard_map/all_gather | solution.py:214
  52.7 6.7 %all_gather.21 = bf16[2,128,256]{2,1,0:T(8,128)(2,1)S(1)} all-gather(bf16[2,128,128]{2,1,0:T(8,128)(2,1)} %param.19), channel_id=1, replica_groups=mesh['chip'=8,'core'=2,'blk'=8,'samp'=2] {'samp'}, dimensions={2}, use_global_device_ids=true | all-gather | bytes 196608 | tf_op jit(solution)/shard_map/all_gather | solution.py:238
  60.9 3.4 %all-to-all-start.1 = ((f32[8,3,8,128]{3,2,1,0:T(8,128)}), f32[8,3,8,128]{3,2,1,0:T(8,128)S(1)}, u32[]{:S(2)}, u32[]{:S(2)}) async-start(f32[8,3,8,128]{3,2,1,0:T(8,128)} %broadcast_in_dim.11), calls=%async_computation.1 | async-start | bytes 196608 | tf_op jit(solution)/shard_map/all_to_all | solution.py:26
  65.7 8.3 %all-to-all-done.1 = f32[8,3,8,128]{3,2,1,0:T(8,128)S(1)} async-done(((f32[8,3,8,128]{3,2,1,0:T(8,128)}), f32[8,3,8,128]{3,2,1,0:T(8,128)S(1)}, u32[]{:S(2)}, u32[]{:S(2)}) %all-to-all-start.1) | async-done | bytes 98336 | tf_op jit(solution)/shard_map/all_to_all | solution.py:26
  74.0 4.6 %all-gather.5.cloned.1.call-done = bf16[32,128,1024]{2,1,0:T(8,128)(2,1)} async-done(((bf16[2,128,1024]{2,1,0:T(8,128)(2,1)}), bf16[32,128,1024]{2,1,0:T(8,128)(2,1)}) %all-gather.5.cloned.1.call-update) | async-done | bytes 8388624 | tf_op jit(solution)/shard_map/all_gather | solution.py:215
  78.6 3.5 %pack_trans.1.mats = bf16[4,8,128,1024]{3,2,1,0:T(8,128)(2,1)S(1)} custom-call(bf16[2,8,2,128,1024]{4,3,2,1,0:T(8,128)(2,1)} %bitcast.26), custom_call_target="tpu_custom_call" | custom-call | tf_op jit(solution)/shard_map/pack_trans/pallas_call | solution.py:220
  82.1 2.6 %forward.8 = (f32[4,8,1024]{2,1,0:T(8,128)S(1)}, f32[8,1024]{1,0:T(8,128)S(1)}) custom-call(f32[8,1024]{1,0:T(8,128)S(1)} %slice_bitcast_fusion.state_ref, f32[2,8,1024]{2,1,0:T(8,128)S(1)} %copy_bitcast_fusion.near_in, f32[2,8,1024]{2,1,0:T(8,128)S(1)} %collective-permute-done.2.far_in, bf16[4,8,128,1024]{3,2,1,0:T(8,128)(2,1)S(1)} %pack_trans.1.mats), custom_call_target="tpu_custom_call" | custom-call | tf_op jit(solution)/shard_map/forward/pallas_call | solution.py:254
  84.8 1.3 collective-permute-start.3
  86.1 1.6 collective-permute-done.3.state_ref
  91.9 43.1 %all-gather.7.cloned.1.call-done = bf16[32,128,1024]{2,1,0:T(8,128)(2,1)} async-done(((bf16[2,128,1024]{2,1,0:T(8,128)(2,1)}), bf16[32,128,1024]{2,1,0:T(8,128)(2,1)}) %all-gather.7.cloned.1.call-update) | async-done | bytes 8388624 | tf_op jit(solution)/shard_map/all_gather | solution.py:215
  134.9 3.7 %pack_smooth.1.mats = bf16[4,8,128,1024]{3,2,1,0:T(8,128)(2,1)S(1)} custom-call(bf16[2,8,2,128,1024]{4,3,2,1,0:T(8,128)(2,1)} %bitcast.25), custom_call_target="tpu_custom_call" | custom-call | tf_op jit(solution)/shard_map/pack_smooth/pallas_call | solution.py:220
  138.6 2.2 %copy-done.1 = bf16[4,8,128,1024]{3,2,1,0:T(8,128)(2,1)S(1)} copy-done((bf16[4,8,128,1024]{3,2,1,0:T(8,128)(2,1)S(1)}, bf16[4,8,128,1024]{3,2,1,0:T(8,128)(2,1)}, u32[]{:S(2)}) %copy-start.1) | copy-done | bytes 8388632
  140.8 0.9 predict.1.pred_ref
  146.0 1.3 collective-permute-start.16
  147.3 47.2 %collective-permute-done.16.state_ref = f32[8,1024]{1,0:T(8,128)S(1)} collective-permute-done((f32[8,1024]{1,0:T(8,128)S(1)}, f32[8,1024]{1,0:T(8,128)S(1)}, u32[]{:S(2)}, u32[]{:S(2)}) %collective-permute-start.16) | collective-permute-done | bytes 32800 | tf_op jit(solution)/shard_map/ppermute | solution.py:289
  194.4 3.3 %backward.15 = (f32[4,8,1024]{2,1,0:T(8,128)S(1)}, f32[8,1024]{1,0:T(8,128)}) custom-call(f32[8,1024]{1,0:T(8,128)S(1)} %collective-permute-done.16.state_ref, f32[4,8,1024]{2,1,0:T(8,128)S(1)} %get-tuple-element.67.filt_ref, f32[4,8,1024]{2,1,0:T(8,128)S(1)} %predict.1.pred_ref, ...), custom_call_target="tpu_custom_call", output_to_operand_aliasing={{0}: (4, {})} | custom-call | tf_op jit(solution)/shard_map/backward/pallas_call | solution.py:278
  (78 shorter events, 15.4 us)
Async XLA Ops:
  6.5 72.1 %all-gather.5.cloned.1.call-start = ((), (), s32[]{:S(2)}) async-start(), calls=%async_computation.2 | async-start | bytes 8912896 | tf_op jit(solution)/shard_map/all_gather | solution.py:215
  17.1 117.8 %all-gather.7.cloned.1.call-start = ((), (), s32[]{:S(2)}) async-start(), calls=%async_computation.3 | async-start | bytes 8912896 | tf_op jit(solution)/shard_map/all_gather | solution.py:215
  18.0 9.7 %collective-permute-start = (f32[2,8,16]{2,1,0:T(8,128)S(1)}, f32[2,8,16]{2,1,0:T(8,128)S(1)}, u32[]{:S(2)}, u32[]{:S(2)}) collective-permute-start(f32[2,8,16]{2,1,0:T(8,128)S(1)} %get-tuple-element.85), channel_id=1, source_target_pairs={{0,2},{2,4},{4,6},{6,8},{8,10},{10,12},{12,14},{14,0},{1,3},{3,5},... | collective-permute-start | bytes 3080 | tf_op jit(solution)/shard_map/ppermute | solution.py:31
  19.9 7.8 %collective-permute-start.1 = (f32[2,8,16]{2,1,0:T(8,128)S(1)}, f32[2,8,16]{2,1,0:T(8,128)S(1)}, u32[]{:S(2)}, u32[]{:S(2)}) collective-permute-start(f32[2,8,16]{2,1,0:T(8,128)S(1)} %get-tuple-element.86), channel_id=1, source_target_pairs={{0,14},{2,0},{4,2},{6,4},{8,6},{10,8},{12,10},{14,12},{1,15},{3,1}... | collective-permute-start | bytes 3080 | tf_op jit(solution)/shard_map/ppermute | solution.py:32
  60.9 13.1 %all-to-all-start.1 = ((f32[8,3,8,128]{3,2,1,0:T(8,128)}), f32[8,3,8,128]{3,2,1,0:T(8,128)S(1)}, u32[]{:S(2)}, u32[]{:S(2)}) async-start(f32[8,3,8,128]{3,2,1,0:T(8,128)} %broadcast_in_dim.11), calls=%async_computation.1 | async-start | bytes 196608 | tf_op jit(solution)/shard_map/all_to_all | solution.py:26
  64.3 0.7 copy-start.3
  74.0 8.1 %collective-permute-start.2 = (f32[2,8,1024]{2,1,0:T(8,128)S(1)}, f32[2,8,1024]{2,1,0:T(8,128)S(1)}, u32[]{:S(2)}, u32[]{:S(2)}) collective-permute-start(f32[2,8,1024]{2,1,0:T(8,128)S(1)} %copy_bitcast_fusion.near_in), channel_id=1, source_target_pairs={{0,16},{16,0},{1,17},{17,1},{2,18},{18,2},{3,19},{19,3},{4,20},{20... | collective-permute-start | bytes 196616 | tf_op jit(solution)/shard_map/ppermute | solution.py:243
  82.1 9.1 %copy-start = (bf16[4,8,128,1024]{3,2,1,0:T(8,128)(2,1)}, bf16[4,8,128,1024]{3,2,1,0:T(8,128)(2,1)S(1)}, u32[]{:S(2)}) copy-start(bf16[4,8,128,1024]{3,2,1,0:T(8,128)(2,1)S(1)} %pack_trans.1.mats) | copy-start | bytes 25165828
  84.8 2.9 %collective-permute-start.3 = (f32[8,1024]{1,0:T(8,128)S(1)}, f32[8,1024]{1,0:T(8,128)S(1)}, u32[]{:S(2)}, u32[]{:S(2)}) collective-permute-start(f32[8,1024]{1,0:T(8,128)S(1)} %get-tuple-element.48), channel_id=1, source_target_pairs={{0,32},{1,33},{2,34},{3,35},{4,36},{5,37},{6,38},{7,39},{8,40},{9,... | collective-permute-start | bytes 98312 | tf_op jit(solution)/shard_map/ppermute | solution.py:268
  87.7 0.7 collective-permute-start.4
  88.4 0.7 collective-permute-start.5
  89.1 0.7 collective-permute-start.6
  89.8 0.7 collective-permute-start.7
  90.5 0.7 collective-permute-start.8
  91.2 47.4 %collective-permute-start.9 = (f32[8,1024]{1,0:T(8,128)S(1)}, f32[8,1024]{1,0:T(8,128)S(1)}, u32[]{:S(2)}, u32[]{:S(2)}) collective-permute-start(f32[8,1024]{1,0:T(8,128)S(1)} %get-tuple-element.60), channel_id=1, source_target_pairs={{192,224},{193,225},{194,226},{195,227},{196,228},{197,229},{198,2... | collective-permute-start | bytes 98312 | tf_op jit(solution)/shard_map/ppermute | solution.py:268
  134.9 5.9 %copy-start.1 = (bf16[4,8,128,1024]{3,2,1,0:T(8,128)(2,1)S(1)}, bf16[4,8,128,1024]{3,2,1,0:T(8,128)(2,1)}, u32[]{:S(2)}) copy-start(bf16[4,8,128,1024]{3,2,1,0:T(8,128)(2,1)} %copy-done) | copy-start | bytes 25165828
  141.7 0.7 collective-permute-start.10
  142.4 0.7 collective-permute-start.11
  143.1 0.7 collective-permute-start.12
  143.8 0.7 collective-permute-start.13
  144.5 0.7 collective-permute-start.14
  145.2 0.7 collective-permute-start.15
  145.9 51.8 %copy-start.2 = (f32[2,8,128]{2,1,0:T(8,128)S(1)}, f32[2,8,128]{2,1,0:T(8,128)}, u32[]{:S(2)}) copy-start(f32[2,8,128]{2,1,0:T(8,128)} %prior_ref.1) | copy-start | bytes 24580
  146.0 48.5 %collective-permute-start.16 = (f32[8,1024]{1,0:T(8,128)S(1)}, f32[8,1024]{1,0:T(8,128)S(1)}, u32[]{:S(2)}, u32[]{:S(2)}) collective-permute-start(f32[8,1024]{1,0:T(8,128)S(1)} %get-tuple-element.82), channel_id=1, source_target_pairs={{32,0},{33,1},{34,2},{35,3},{36,4},{37,5},{38,6},{39,7},{40,8},{41... | collective-permute-start | bytes 98312 | tf_op jit(solution)/shard_map/ppermute | solution.py:289
Sparse Core Ops, SparseCore 0:
  17.2 61.3 all-gather.4
  80.4 54.4 all-gather.6

commit v3 on v2

--- a/solution.py
+++ b/solution.py
@@ -62,22 +62,21 @@
     return value[:rows] + value[rows:]
 
 
-def pack_kernel(parts, rows_ref, out_ref, sems):
-    cores, count, steps = rows_ref.shape[:3]
-    copies = []
-    for core in range(cores):
-        for step in range(steps):
-            for part in range(parts):
-                blocks = pl.ds(part * (count // parts), count // parts)
-                copy = pltpu.make_async_copy(
-                    rows_ref.at[core, blocks, step],
-                    out_ref.at[core * steps + step, blocks],
-                    sems.at[len(copies)],
-                )
-                copy.start()
-                copies.append(copy)
-    for copy in copies:
-        copy.wait()
+def start_pack(rows_ref, mats_ref, sems, order):
+    steps, started = rows_ref.shape[2], {}
+    for turn in order:
+        started[turn] = []
+        for part in range(sems.shape[1]):
+            size = rows_ref.shape[1] // sems.shape[1]
+            blocks = pl.ds(part * size, size)
+            copy = pltpu.make_async_copy(
+                rows_ref.at[turn // steps, blocks, turn % steps],
+                mats_ref.at[turn, blocks],
+                sems.at[turn, part],
+            )
+            copy.start()
+            started[turn].append(copy)
+    return started
 
 
 def apply_rows(mats, turn, value, store):
@@ -89,46 +88,96 @@
         store(slice(k * rows, (k + 2) * rows), joined_rows(part))
 
 
-def forward_kernel(hop, state_ref, near_in, far_in, mats, *refs):
-    filt_ref, sent_ref = refs[-2:]
-
+def apply_columns(flipped, turn, value, store):
+    terms = split_rows(value)
+    for k in range(0, flipped.shape[2], 512):
+        columns = slice(k, k + 512)
+        part = jnp.dot(terms, flipped[turn, :, columns], preferred_element_type=f32)
+        store(columns, joined_rows(part))
+
+
+def flip_kernel(mats_ref, out_ref):
+    rows = mats_ref.shape[2]
+
+    def step(turn, carry):
+        for k in range(0, mats_ref.shape[1], 2):
+            block = jnp.concatenate([mats_ref[turn, k], mats_ref[turn, k + 1]], axis=0)
+            for j in range(0, block.shape[1], 256):
+                out_ref[turn, j : j + 256, k * rows : (k + 2) * rows] = block[:, j : j + 256].T
+        return carry
+
+    lax.fori_loop(0, mats_ref.shape[0], step, 0)
+
+
+def forward_step(apply, mats, turn, near_in, far_in, filt_ref, sent_ref):
+    is_near = turn // 2 == lax.axis_index("core")
+
+    def store(columns, part):
+        at = lax.rem(turn, 2)
+        added = jnp.where(is_near, near_in[at, :, columns], far_in[at, :, columns])
+        filt_ref[turn, :, columns] = part + added
+
+    apply(mats, turn, sent_ref[...], store)
+    sent_ref[...] = filt_ref[turn]
+
+
+def forward_first_kernel(state_ref, near_in, far_in, rows_ref, mats_ref, filt_ref, sent_ref, sems):
+    copies = start_pack(rows_ref, mats_ref, sems, range(4))
+    sent_ref[...] = state_ref[...]
+    for turn in range(4):
+        for copy in copies[turn]:
+            copy.wait()
+
+        @pl.when(lax.axis_index("chip") == 0)
+        def _():
+            at = jnp.int32(turn)
+            forward_step(apply_rows, mats_ref, at, near_in, far_in, filt_ref, sent_ref)
+
+
+def forward_kernel(hop, state_ref, near_in, far_in, mats, held_ref, filt_ref, sent_ref):
     @pl.when(lax.axis_index("chip") == hop)
     def _():
         sent_ref[...] = state_ref[...]
 
         def step(turn, carry):
-            is_near = turn // 2 == lax.axis_index("core")
-
-            def store(columns, part):
-                at = lax.rem(turn, 2)
-                added = jnp.where(is_near, near_in[at, :, columns], far_in[at, :, columns])
-                filt_ref[turn, :, columns] = part + added
-
-            apply_rows(mats, turn, sent_ref[...], store)
-            sent_ref[...] = filt_ref[turn]
+            forward_step(apply_columns, mats, turn, near_in, far_in, filt_ref, sent_ref)
             return carry
 
         lax.fori_loop(0, 4, step, 0)
 
 
-def backward_kernel(hop, hops, state_ref, filt_ref, pred_ref, mats, *refs):
-    target_ref, sent_ref = refs[-2:]
-
+def backward_step(apply, mats, turn, filt_ref, pred_ref, out_ref, sent_ref):
+    def store(columns, part):
+        out_ref[turn, :, columns] = filt_ref[turn, :, columns] + part
+
+    apply(mats, turn, sent_ref[...] - pred_ref[turn], store)
+    sent_ref[...] = out_ref[turn]
+
+
+def backward_first_kernel(filt_ref, pred_ref, rows_ref, mats_ref, out_ref, sent_ref, sems):
+    copies = start_pack(rows_ref, mats_ref, sems, (2, 1, 0, 3))
+    out_ref[3] = filt_ref[3]
+    sent_ref[...] = filt_ref[3]
+    for turn in (2, 1, 0):
+        for copy in copies[turn]:
+            copy.wait()
+
+        @pl.when(lax.axis_index("chip") == lax.axis_size("chip") - 1)
+        def _():
+            at = jnp.int32(turn)
+            backward_step(apply_rows, mats_ref, at, filt_ref, pred_ref, out_ref, sent_ref)
+
+    for copy in copies[3]:
+        copy.wait()
+
+
+def backward_kernel(hop, state_ref, filt_ref, pred_ref, mats, held_ref, out_ref, sent_ref):
     @pl.when(lax.axis_index("chip") == hop)
     def _():
         sent_ref[...] = state_ref[...]
 
         def step(i, carry):
-            turn = 3 - i
-            change = sent_ref[...] - pred_ref[turn]
-            if hop == hops - 1:
-                change = jnp.where(turn == 3, 0.0, change)
-
-            def store(columns, part):
-                target_ref[turn, :, columns] = filt_ref[turn, :, columns] + part
-
-            apply_rows(mats, turn, change, store)
-            sent_ref[...] = target_ref[turn]
+            backward_step(apply_columns, mats, 3 - i, filt_ref, pred_ref, out_ref, sent_ref)
             return carry
 
         lax.fori_loop(0, 4, step, 0)
@@ -215,16 +264,9 @@
         rows = lax.all_gather(whole, ("core", "blk"), axis=0)
         return rows.reshape((2, cycle) + rows.shape[1:])
 
-    def pack(rows, name):
-        parts = 4
-        made = call(
-            functools.partial(pack_kernel, parts),
-            name,
-            mats_shape,
-            [HBM],
-            [pltpu.SemaphoreType.DMA((4 * parts,))],
-        )(in_hbm(rows))
-        return in_vmem(made)
+    def flip(mats, name):
+        shape = jax.ShapeDtypeStruct((4, state_count, state_count), bf16)
+        return in_vmem(call(flip_kernel, name, shape, [VMEM])(mats))
 
     trans_rows = all_rows(trans_mats)
 
@@ -242,52 +284,41 @@
     near_in, start = gathered[:step_count], gathered[step_count]
     far_in = lax.ppermute(near_in, "core", swapped(2))
     trans_rows, near_in = lax.optimization_barrier((trans_rows, near_in))
-    trans = pack(trans_rows, "pack_trans")
 
     smooth_mats, _ = lax.optimization_barrier((smooth_mats, all_resid))
     smooth_rows = all_rows(smooth_mats)
 
     filt_shape = jax.ShapeDtypeStruct((4, sample_count, state_count), f32)
     state_shape = jax.ShapeDtypeStruct((sample_count, state_count), f32)
-
-    def forward(hop, state, *filtered):
-        return call(
-            functools.partial(forward_kernel, hop),
-            "forward",
-            (filt_shape, state_shape),
-            [VMEM] * (4 + len(filtered)),
-            (),
-            {4: 0} if filtered else None,
-        )(state, near_in, far_in, trans, *filtered)
 
     kron_shape = jax.ShapeDtypeStruct((128, 128), f32)
     kron = in_vmem(call(kron_kernel, "kron", kron_shape, [SMEM])(site_trans))
     kron, start = lax.optimization_barrier((kron, start))
-    filtered, sent = forward(0, start)
+    dmas = [pltpu.SemaphoreType.DMA((4, 4))]
+    shapes = (mats_shape, filt_shape, state_shape)
+    trans, filtered, sent = call(
+        forward_first_kernel, "forward_first", shapes, [VMEM] * 3 + [HBM], dmas
+    )(start, near_in, far_in, in_hbm(trans_rows))
+    trans = flip(in_vmem(trans), "flip_trans")
     for hop in range(1, groups):
         state = lax.ppermute(sent, "chip", [(hop - 1, hop)])
-        if hop == groups - 1:
-            smooth_rows, filtered = lax.optimization_barrier((smooth_rows, filtered))
-            smooth = pack(smooth_rows, "pack_smooth")
-            filtered, smooth = lax.optimization_barrier((filtered, smooth))
-        filtered, sent = forward(hop, state, filtered)
+        kernel = functools.partial(forward_kernel, hop)
+        filtered, sent = call(kernel, "forward", shapes[1:], [VMEM] * 5, (), {4: 0})(
+            state, near_in, far_in, trans, filtered
+        )
 
     predicted = call(predict_kernel, "predict", filt_shape, [VMEM, VMEM])(kron, filtered)
-
-    def backward(hop, state, *smoothed):
-        return call(
-            functools.partial(backward_kernel, hop, groups),
-            "backward",
-            (filt_shape, state_shape),
-            [VMEM] * (4 + len(smoothed)),
-            (),
-            {4: 0} if smoothed else None,
-        )(state, filtered, predicted, smooth, *smoothed)
-
-    smoothed, sent = backward(groups - 1, sent)
+    smooth_rows, predicted = lax.optimization_barrier((smooth_rows, predicted))
+    smooth, smoothed, sent = call(
+        backward_first_kernel, "backward_first", shapes, [VMEM] * 2 + [HBM], dmas
+    )(filtered, predicted, in_hbm(smooth_rows))
+    smooth = flip(in_vmem(smooth), "flip_smooth")
     for hop in range(groups - 2, -1, -1):
         state = lax.ppermute(sent, "chip", [(hop + 1, hop)])
-        smoothed, sent = backward(hop, state, smoothed)
+        kernel = functools.partial(backward_kernel, hop)
+        smoothed, sent = call(kernel, "backward", shapes[1:], [VMEM] * 5, (), {4: 0})(
+            state, filtered, predicted, smooth, smoothed
+        )
     out_shape = jax.ShapeDtypeStruct(prior_path.shape, f32)
     return call(finish_kernel, "finish", out_shape, [VMEM, VMEM])(prior_path, smoothed)
 

time: 206 us -> 191 us (0.927)
  waiting for transfers between devices: 105 us -> 88.4 us
  Pallas kernels: 15.4 us -> 18.1 us
  local copies, waits for them, and re-layouts: 7.3 us -> 5.12 us
    ppermute x7, waiting for transfers between devices: 47.2 us -> 34.4 us  [on_device(): state = lax.ppermute(sent, 'chip', [(hop + 1, hop)])]
    pallas_call x18, Pallas kernels: 13.3 us -> 15.9 us  [the longest x2 5.05 us: flip(): return in_vmem(call(flip_kernel, name, shape, [VMEM])(mats))]
    unnamed x13 -> x9, local copies, waits for them, and re-layouts: 4.78 us -> 2.59 us
  transfers between devices with their start and end apart: 20 -> 20, of which waited for: 5 -> 4; matrix products, arithmetic and copies ran while one was open for 4% -> 4% of each run, Pallas kernels for 5% -> 6%
where the time goes in v3:
time: 191 us
  waiting for transfers between devices  88.4 us (46%)
  blocking collectives  39.8 us (21%)
  starting transfers between devices  21.1 us (11%)
  Pallas kernels  18.1 us (9%)
  between operations  13.9 us (7%)
  local copies, waits for them, and re-layouts  5.12 us (3%)
  other arithmetic  3.03 us (2%)
    all_gather x2, waiting for transfers between devices, all_rows(): rows = lax.all_gather(whole, ('core', 'blk'), axis=0)  45.7 us
    ppermute x7, waiting for transfers between devices, on_device(): state = lax.ppermute(sent, 'chip', [(hop + 1, hop)])  34.4 us
    all_gather x2, blocking collectives, all_rows(): whole = lax.all_gather(mats, 'samp', axis=2, tiled=True)  19.5 us
    all_to_all x1, blocking collectives, all_blocks(): return lax.all_to_all(copies, axis, 0, 0, tiled=True)  13.6 us
    all_to_all x1, waiting for transfers between devices, all_blocks(): return lax.all_to_all(copies, axis, 0, 0, tiled=True)  8.32 us
    all_gather x1, blocking collectives, on_device(): gain = lax.all_gather(gain_mats, 'samp', axis=2, tiled=True)  6.68 us
    ppermute x7, starting transfers between devices, on_device(): state = lax.ppermute(sent, 'chip', [(hop - 1, hop)])  6.55 us
    ppermute x7, starting transfers between devices, on_device(): state = lax.ppermute(sent, 'chip', [(hop + 1, hop)])  5.27 us
  transfers between devices with their start and end apart: 20, of which 4 were waited for; matrix products, arithmetic and copies ran while one was open for 4% of the time, Pallas kernels for 6%

profile of v3, /device:TPU:16, one launch (start us, length us, event | category | flops | bytes accessed | tf_op | source)
XLA Modules:
  0.0 190.5 jit_solution(8788343057524953040)
XLA Ops:
  6.5 10.5 %all_gather.22 = bf16[2,128,1024]{2,1,0:T(8,128)(2,1)} all-gather(bf16[2,128,512]{2,1,0:T(8,128)(2,1)} %param.18), channel_id=1, replica_groups=mesh['chip'=8,'core'=2,'blk'=8,'samp'=2] {'samp'}, dimensions={2}, use_global_device_ids=true | all-gather | bytes 786432 | tf_op jit(solution)/shard_map/all_gather | solution.py:263
  17.1 0.8 fusion.10
  18.0 1.9 %collective-permute-start = (f32[2,8,16]{2,1,0:T(8,128)S(1)}, f32[2,8,16]{2,1,0:T(8,128)S(1)}, u32[]{:S(2)}, u32[]{:S(2)}) collective-permute-start(f32[2,8,16]{2,1,0:T(8,128)S(1)} %get-tuple-element.83), channel_id=1, source_target_pairs={{0,2},{2,4},{4,6},{6,8},{8,10},{10,12},{12,14},{14,0},{1,3},{3,5},... | collective-permute-start | bytes 3080 | tf_op jit(solution)/shard_map/ppermute | solution.py:31
  19.9 4.0 %collective-permute-start.1 = (f32[2,8,16]{2,1,0:T(8,128)S(1)}, f32[2,8,16]{2,1,0:T(8,128)S(1)}, u32[]{:S(2)}, u32[]{:S(2)}) collective-permute-start(f32[2,8,16]{2,1,0:T(8,128)S(1)} %get-tuple-element.84), channel_id=1, source_target_pairs={{0,14},{2,0},{4,2},{6,4},{8,6},{10,8},{12,10},{14,12},{1,15},{3,1}... | collective-permute-start | bytes 3080 | tf_op jit(solution)/shard_map/ppermute | solution.py:32
  23.9 0.8 copy.42
  25.9 0.8 copy.40
  27.7 0.9 fusion
  28.7 13.6 %all_to_all.10 = f32[8,1,512]{2,1,0:T(1,128)S(1)} all-to-all(f32[8,1,512]{2,1,0:T(1,128)S(1)} %reshape.49), channel_id=1, replica_groups=mesh['chip'=8,'core'=2,'blk'=8,'samp'=2] {'blk'}, dimensions={0} | all-to-all | bytes 32768 | tf_op jit(solution)/shard_map/all_to_all | solution.py:26
  43.7 9.0 %all_gather.25 = bf16[2,128,1024]{2,1,0:T(8,128)(2,1)} all-gather(bf16[2,128,512]{2,1,0:T(8,128)(2,1)} %param.20), channel_id=1, replica_groups=mesh['chip'=8,'core'=2,'blk'=8,'samp'=2] {'samp'}, dimensions={2}, use_global_device_ids=true | all-gather | bytes 786432 | tf_op jit(solution)/shard_map/all_gather | solution.py:263
  52.7 6.7 %all_gather.21 = bf16[2,128,256]{2,1,0:T(8,128)(2,1)S(1)} all-gather(bf16[2,128,128]{2,1,0:T(8,128)(2,1)} %param.19), channel_id=1, replica_groups=mesh['chip'=8,'core'=2,'blk'=8,'samp'=2] {'samp'}, dimensions={2}, use_global_device_ids=true | all-gather | bytes 196608 | tf_op jit(solution)/shard_map/all_gather | solution.py:280
  59.6 0.7 pad_maximum_fusion
  61.0 3.4 %all-to-all-start.1 = ((f32[8,3,8,128]{3,2,1,0:T(8,128)}), f32[8,3,8,128]{3,2,1,0:T(8,128)S(1)}, u32[]{:S(2)}, u32[]{:S(2)}) async-start(f32[8,3,8,128]{3,2,1,0:T(8,128)} %broadcast_in_dim.11), calls=%async_computation.1 | async-start | bytes 196608 | tf_op jit(solution)/shard_map/all_to_all | solution.py:26
  65.7 8.3 %all-to-all-done.1 = f32[8,3,8,128]{3,2,1,0:T(8,128)S(1)} async-done(((f32[8,3,8,128]{3,2,1,0:T(8,128)}), f32[8,3,8,128]{3,2,1,0:T(8,128)S(1)}, u32[]{:S(2)}, u32[]{:S(2)}) %all-to-all-start.1) | async-done | bytes 98336 | tf_op jit(solution)/shard_map/all_to_all | solution.py:26
  74.1 4.6 %all-gather.5.cloned.1.call-done = bf16[32,128,1024]{2,1,0:T(8,128)(2,1)} async-done(((bf16[2,128,1024]{2,1,0:T(8,128)(2,1)}), bf16[32,128,1024]{2,1,0:T(8,128)(2,1)}) %all-gather.5.cloned.1.call-update) | async-done | bytes 8388624 | tf_op jit(solution)/shard_map/all_gather | solution.py:264
  78.6 4.3 %forward_first.1 = (bf16[4,8,128,1024]{3,2,1,0:T(8,128)(2,1)S(1)}, f32[4,8,1024]{2,1,0:T(8,128)S(1)}, f32[8,1024]{1,0:T(8,128)S(1)}) custom-call(f32[8,1024]{1,0:T(8,128)S(1)} %slice_bitcast_fusion.state_ref, f32[2,8,1024]{2,1,0:T(8,128)S(1)} %copy_bitcast_fusion.near_in, f32[2,8,1024]{2,1,0:T(8,128)S(1)} %collective-permute-done.2.far_in, ...), custom_call_target="tpu_custom_call" | custom-call | tf_op jit(solution)/shard_map/forward_first/pallas_call | solution.py:299
  83.0 2.6 %collective-permute-start.3 = (f32[8,1024]{1,0:T(8,128)S(1)}, f32[8,1024]{1,0:T(8,128)S(1)}, u32[]{:S(2)}, u32[]{:S(2)}) collective-permute-start(f32[8,1024]{1,0:T(8,128)S(1)} %get-tuple-element.47), channel_id=1, source_target_pairs={{0,32},{1,33},{2,34},{3,35},{4,36},{5,37},{6,38},{7,39},{8,40},{9,... | collective-permute-start | bytes 98312 | tf_op jit(solution)/shard_map/ppermute | solution.py:304
  85.5 2.5 %flip_trans.1.mats = bf16[4,1024,1024]{2,1,0:T(8,128)(2,1)S(1)} custom-call(bf16[4,8,128,1024]{3,2,1,0:T(8,128)(2,1)S(1)} %get-tuple-element.48.mats_ref), custom_call_target="tpu_custom_call" | custom-call | tf_op jit(solution)/shard_map/flip_trans/pallas_call | solution.py:269
  92.9 0.9 predict.1.pred_ref
  93.8 41.1 %all-gather.7.cloned.1.call-done = bf16[32,128,1024]{2,1,0:T(8,128)(2,1)} async-done(((bf16[2,128,1024]{2,1,0:T(8,128)(2,1)}), bf16[32,128,1024]{2,1,0:T(8,128)(2,1)}) %all-gather.7.cloned.1.call-update) | async-done | bytes 8388624 | tf_op jit(solution)/shard_map/all_gather | solution.py:264
  135.0 3.5 %backward_first.1 = (bf16[4,8,128,1024]{3,2,1,0:T(8,128)(2,1)S(1)}, f32[4,8,1024]{2,1,0:T(8,128)S(1)}, f32[8,1024]{1,0:T(8,128)S(1)}) custom-call(f32[4,8,1024]{2,1,0:T(8,128)S(1)} %get-tuple-element.62.filt_ref, f32[4,8,1024]{2,1,0:T(8,128)S(1)} %predict.1.pred_ref, bf16[2,8,2,128,1024]{4,3,2,1,0:T(8,128)(2,1)} %bitcast.25), custom_call_target="tpu_custom_call" | custom-call | tf_op jit(solution)/shard_map/backward_first/pallas_call | solution.py:312
  139.2 2.5 %flip_smooth.1.mats = bf16[4,1024,1024]{2,1,0:T(8,128)(2,1)S(1)} custom-call(bf16[4,8,128,1024]{3,2,1,0:T(8,128)(2,1)S(1)} %get-tuple-element.68.mats_ref), custom_call_target="tpu_custom_call" | custom-call | tf_op jit(solution)/shard_map/flip_smooth/pallas_call | solution.py:269
  145.3 1.3 collective-permute-start.16
  146.6 34.3 %collective-permute-done.16.state_ref = f32[8,1024]{1,0:T(8,128)S(1)} collective-permute-done((f32[8,1024]{1,0:T(8,128)S(1)}, f32[8,1024]{1,0:T(8,128)S(1)}, u32[]{:S(2)}, u32[]{:S(2)}) %collective-permute-start.16) | collective-permute-done | bytes 32800 | tf_op jit(solution)/shard_map/ppermute | solution.py:317
  180.9 2.2 %backward.13 = (f32[4,8,1024]{2,1,0:T(8,128)S(1)}, f32[8,1024]{1,0:T(8,128)}) custom-call(f32[8,1024]{1,0:T(8,128)S(1)} %collective-permute-done.16.state_ref, f32[4,8,1024]{2,1,0:T(8,128)S(1)} %get-tuple-element.62.filt_ref, f32[4,8,1024]{2,1,0:T(8,128)S(1)} %predict.1.pred_ref, ...), custom_call_target="tpu_custom_call", output_to_operand_aliasing={{0}: (4, {})} | custom-call | tf_op jit(solution)/shard_map/backward/pallas_call | solution.py:319
  (74 shorter events, 15.3 us)
Async XLA Ops:
  6.5 72.1 %all-gather.5.cloned.1.call-start = ((), (), s32[]{:S(2)}) async-start(), calls=%async_computation.2 | async-start | bytes 8912896 | tf_op jit(solution)/shard_map/all_gather | solution.py:264
  17.1 117.9 %all-gather.7.cloned.1.call-start = ((), (), s32[]{:S(2)}) async-start(), calls=%async_computation.3 | async-start | bytes 8912896 | tf_op jit(solution)/shard_map/all_gather | solution.py:264
  18.0 9.7 %collective-permute-start = (f32[2,8,16]{2,1,0:T(8,128)S(1)}, f32[2,8,16]{2,1,0:T(8,128)S(1)}, u32[]{:S(2)}, u32[]{:S(2)}) collective-permute-start(f32[2,8,16]{2,1,0:T(8,128)S(1)} %get-tuple-element.83), channel_id=1, source_target_pairs={{0,2},{2,4},{4,6},{6,8},{8,10},{10,12},{12,14},{14,0},{1,3},{3,5},... | collective-permute-start | bytes 3080 | tf_op jit(solution)/shard_map/ppermute | solution.py:31
  19.9 7.8 %collective-permute-start.1 = (f32[2,8,16]{2,1,0:T(8,128)S(1)}, f32[2,8,16]{2,1,0:T(8,128)S(1)}, u32[]{:S(2)}, u32[]{:S(2)}) collective-permute-start(f32[2,8,16]{2,1,0:T(8,128)S(1)} %get-tuple-element.84), channel_id=1, source_target_pairs={{0,14},{2,0},{4,2},{6,4},{8,6},{10,8},{12,10},{14,12},{1,15},{3,1}... | collective-permute-start | bytes 3080 | tf_op jit(solution)/shard_map/ppermute | solution.py:32
  61.0 13.1 %all-to-all-start.1 = ((f32[8,3,8,128]{3,2,1,0:T(8,128)}), f32[8,3,8,128]{3,2,1,0:T(8,128)S(1)}, u32[]{:S(2)}, u32[]{:S(2)}) async-start(f32[8,3,8,128]{3,2,1,0:T(8,128)} %broadcast_in_dim.11), calls=%async_computation.1 | async-start | bytes 196608 | tf_op jit(solution)/shard_map/all_to_all | solution.py:26
  64.3 0.7 copy-start.1
  74.0 4.6 %collective-permute-start.2 = (f32[2,8,1024]{2,1,0:T(8,128)S(1)}, f32[2,8,1024]{2,1,0:T(8,128)S(1)}, u32[]{:S(2)}, u32[]{:S(2)}) collective-permute-start(f32[2,8,1024]{2,1,0:T(8,128)S(1)} %copy_bitcast_fusion.near_in), channel_id=1, source_target_pairs={{0,16},{16,0},{1,17},{17,1},{2,18},{18,2},{3,19},{19,3},{4,20},{20... | collective-permute-start | bytes 196616 | tf_op jit(solution)/shard_map/ppermute | solution.py:285
  83.0 5.1 %collective-permute-start.3 = (f32[8,1024]{1,0:T(8,128)S(1)}, f32[8,1024]{1,0:T(8,128)S(1)}, u32[]{:S(2)}, u32[]{:S(2)}) collective-permute-start(f32[8,1024]{1,0:T(8,128)S(1)} %get-tuple-element.47), channel_id=1, source_target_pairs={{0,32},{1,33},{2,34},{3,35},{4,36},{5,37},{6,38},{7,39},{8,40},{9,... | collective-permute-start | bytes 98312 | tf_op jit(solution)/shard_map/ppermute | solution.py:304
  88.1 0.7 collective-permute-start.4
  88.8 0.7 collective-permute-start.5
  89.5 0.7 collective-permute-start.6
  90.2 0.7 collective-permute-start.7
  90.9 0.7 collective-permute-start.8
  91.6 0.7 collective-permute-start.9
  138.5 3.2 %collective-permute-start.10 = (f32[8,1024]{1,0:T(8,128)S(1)}, f32[8,1024]{1,0:T(8,128)S(1)}, u32[]{:S(2)}, u32[]{:S(2)}) collective-permute-start(f32[8,1024]{1,0:T(8,128)S(1)} %get-tuple-element.67), channel_id=1, source_target_pairs={{224,192},{225,193},{226,194},{227,195},{228,196},{229,197},{230,1... | collective-permute-start | bytes 98312 | tf_op jit(solution)/shard_map/ppermute | solution.py:317
  141.7 0.7 collective-permute-start.11
  142.4 0.7 collective-permute-start.12
  143.1 0.7 collective-permute-start.13
  143.8 0.7 collective-permute-start.14
  144.6 0.7 collective-permute-start.15
  145.2 37.9 %copy-start = (f32[2,8,128]{2,1,0:T(8,128)S(1)}, f32[2,8,128]{2,1,0:T(8,128)}, u32[]{:S(2)}) copy-start(f32[2,8,128]{2,1,0:T(8,128)} %prior_ref.1) | copy-start | bytes 24580
  145.3 35.6 %collective-permute-start.16 = (f32[8,1024]{1,0:T(8,128)S(1)}, f32[8,1024]{1,0:T(8,128)S(1)}, u32[]{:S(2)}, u32[]{:S(2)}) collective-permute-start(f32[8,1024]{1,0:T(8,128)S(1)} %get-tuple-element.80), channel_id=1, source_target_pairs={{32,0},{33,1},{34,2},{35,3},{36,4},{37,5},{38,6},{39,7},{40,8},{41... | collective-permute-start | bytes 98312 | tf_op jit(solution)/shard_map/ppermute | solution.py:317
Sparse Core Ops, SparseCore 0:
  17.2 61.3 all-gather.4
  80.5 54.4 all-gather.6

commit v4 on v3

--- a/solution.py
+++ b/solution.py
@@ -10,6 +10,7 @@
 bf16, f32 = jnp.bfloat16, jnp.float32
 ROWS_BY_ROWS = (((1,), (1,)), ((), ()))
 VMEM_LIMIT = 2 * 1024 * 1024
+CHUNK = 256
 
 
 def ring(count, step):
@@ -88,12 +89,22 @@
         store(slice(k * rows, (k + 2) * rows), joined_rows(part))
 
 
-def apply_columns(flipped, turn, value, store):
-    terms = split_rows(value)
-    for k in range(0, flipped.shape[2], 512):
-        columns = slice(k, k + 512)
-        part = jnp.dot(terms, flipped[turn, :, columns], preferred_element_type=f32)
-        store(columns, joined_rows(part))
+def in_chunks(ref):
+    return [slice(k, k + CHUNK) for k in range(0, ref.shape[-1], CHUNK)]
+
+
+def apply_columns(flipped, turn, values):
+    terms = [split_rows(value) for value in values]
+    chunks = in_chunks(flipped)
+    return [
+        joined_rows(
+            sum(
+                jnp.dot(term, flipped[turn, rows, columns], preferred_element_type=f32)
+                for term, rows in zip(terms, chunks)
+            )
+        )
+        for columns in chunks
+    ]
 
 
 def flip_kernel(mats_ref, out_ref):
@@ -137,13 +148,17 @@
 def forward_kernel(hop, state_ref, near_in, far_in, mats, held_ref, filt_ref, sent_ref):
     @pl.when(lax.axis_index("chip") == hop)
     def _():
-        sent_ref[...] = state_ref[...]
-
-        def step(turn, carry):
-            forward_step(apply_columns, mats, turn, near_in, far_in, filt_ref, sent_ref)
-            return carry
-
-        lax.fori_loop(0, 4, step, 0)
+        chunks = in_chunks(state_ref)
+        state = [state_ref[:, columns] for columns in chunks]
+        first = lax.axis_index("core") == 0
+        for turn in range(4):
+            parts = apply_columns(mats, turn, state)
+            for n, columns in enumerate(chunks):
+                inputs = (near_in[turn % 2, :, columns], far_in[turn % 2, :, columns])
+                state[n] = parts[n] + jnp.where(first, *(inputs if turn < 2 else inputs[::-1]))
+                filt_ref[turn, :, columns] = state[n]
+                if turn == 3:
+                    sent_ref[:, columns] = state[n]
 
 
 def backward_step(apply, mats, turn, filt_ref, pred_ref, out_ref, sent_ref):
@@ -174,13 +189,16 @@
 def backward_kernel(hop, state_ref, filt_ref, pred_ref, mats, held_ref, out_ref, sent_ref):
     @pl.when(lax.axis_index("chip") == hop)
     def _():
-        sent_ref[...] = state_ref[...]
-
-        def step(i, carry):
-            backward_step(apply_columns, mats, 3 - i, filt_ref, pred_ref, out_ref, sent_ref)
-            return carry
-
-        lax.fori_loop(0, 4, step, 0)
+        chunks = in_chunks(state_ref)
+        state = [state_ref[:, columns] for columns in chunks]
+        for turn in range(3, -1, -1):
+            change = [state[n] - pred_ref[turn, :, columns] for n, columns in enumerate(chunks)]
+            parts = apply_columns(mats, turn, change)
+            for n, columns in enumerate(chunks):
+                state[n] = filt_ref[turn, :, columns] + parts[n]
+                out_ref[turn, :, columns] = state[n]
+                if turn == 0:
+                    sent_ref[:, columns] = state[n]
 
 
 def finish_kernel(prior_ref, smooth_ref, out_ref):

time: 191 us -> 189 us (0.990)
  waiting for transfers between devices: 88.4 us -> 86.4 us
  transfers between devices with their start and end apart: 20 -> 20, of which waited for: 4 -> 4; matrix products, arithmetic and copies ran while one was open for 4% -> 5% of each run, Pallas kernels for 6% -> 6%
where the time goes in v4:
time: 189 us; the launch traced here: 188 us
  waiting for transfers between devices  86.4 us (46%)
  blocking collectives  39.8 us (21%)
  starting transfers between devices  21.1 us (11%)
  Pallas kernels  18 us (10%)
  between operations  13.9 us (7%)
  local copies, waits for them, and re-layouts  5.12 us (3%)
  other arithmetic  3.03 us (2%)
    all_gather x2, waiting for transfers between devices, all_rows(): rows = lax.all_gather(whole, ('core', 'blk'), axis=0)  45.5 us
    ppermute x7, waiting for transfers between devices, on_device(): state = lax.ppermute(sent, 'chip', [(hop + 1, hop)])  32.6 us
    all_gather x2, blocking collectives, all_rows(): whole = lax.all_gather(mats, 'samp', axis=2, tiled=True)  19.5 us
    all_to_all x1, blocking collectives, all_blocks(): return lax.all_to_all(copies, axis, 0, 0, tiled=True)  13.6 us
    all_to_all x1, waiting for transfers between devices, all_blocks(): return lax.all_to_all(copies, axis, 0, 0, tiled=True)  8.32 us
    all_gather x1, blocking collectives, on_device(): gain = lax.all_gather(gain_mats, 'samp', axis=2, tiled=True)  6.68 us
    ppermute x7, starting transfers between devices, on_device(): state = lax.ppermute(sent, 'chip', [(hop - 1, hop)])  6.55 us
    ppermute x7, starting transfers between devices, on_device(): state = lax.ppermute(sent, 'chip', [(hop + 1, hop)])  5.27 us
  transfers between devices with their start and end apart: 20, of which 4 were waited for; matrix products, arithmetic and copies ran while one was open for 5% of the time, Pallas kernels for 6%

profile of v4, /device:TPU:16, one launch (start us, length us, event | category | flops | bytes accessed | tf_op | source)
XLA Modules:
  0.0 188.4 jit_solution(8941346062123713418)
XLA Ops:
  6.5 10.5 %all_gather.22 = bf16[2,128,1024]{2,1,0:T(8,128)(2,1)} all-gather(bf16[2,128,512]{2,1,0:T(8,128)(2,1)} %param.18), channel_id=1, replica_groups=mesh['chip'=8,'core'=2,'blk'=8,'samp'=2] {'samp'}, dimensions={2}, use_global_device_ids=true | all-gather | bytes 786432 | tf_op jit(solution)/shard_map/all_gather | solution.py:281
  17.1 0.8 fusion.10
  18.0 1.9 %collective-permute-start = (f32[2,8,16]{2,1,0:T(8,128)S(1)}, f32[2,8,16]{2,1,0:T(8,128)S(1)}, u32[]{:S(2)}, u32[]{:S(2)}) collective-permute-start(f32[2,8,16]{2,1,0:T(8,128)S(1)} %get-tuple-element.83), channel_id=1, source_target_pairs={{0,2},{2,4},{4,6},{6,8},{8,10},{10,12},{12,14},{14,0},{1,3},{3,5},... | collective-permute-start | bytes 3080 | tf_op jit(solution)/shard_map/ppermute | solution.py:32
  19.9 4.0 %collective-permute-start.1 = (f32[2,8,16]{2,1,0:T(8,128)S(1)}, f32[2,8,16]{2,1,0:T(8,128)S(1)}, u32[]{:S(2)}, u32[]{:S(2)}) collective-permute-start(f32[2,8,16]{2,1,0:T(8,128)S(1)} %get-tuple-element.84), channel_id=1, source_target_pairs={{0,14},{2,0},{4,2},{6,4},{8,6},{10,8},{12,10},{14,12},{1,15},{3,1}... | collective-permute-start | bytes 3080 | tf_op jit(solution)/shard_map/ppermute | solution.py:33
  23.9 0.8 copy.42
  25.9 0.8 copy.40
  27.7 0.9 fusion
  28.7 13.6 %all_to_all.10 = f32[8,1,512]{2,1,0:T(1,128)S(1)} all-to-all(f32[8,1,512]{2,1,0:T(1,128)S(1)} %reshape.49), channel_id=1, replica_groups=mesh['chip'=8,'core'=2,'blk'=8,'samp'=2] {'blk'}, dimensions={0} | all-to-all | bytes 32768 | tf_op jit(solution)/shard_map/all_to_all | solution.py:27
  43.7 9.0 %all_gather.25 = bf16[2,128,1024]{2,1,0:T(8,128)(2,1)} all-gather(bf16[2,128,512]{2,1,0:T(8,128)(2,1)} %param.20), channel_id=1, replica_groups=mesh['chip'=8,'core'=2,'blk'=8,'samp'=2] {'samp'}, dimensions={2}, use_global_device_ids=true | all-gather | bytes 786432 | tf_op jit(solution)/shard_map/all_gather | solution.py:281
  52.7 6.7 %all_gather.21 = bf16[2,128,256]{2,1,0:T(8,128)(2,1)S(1)} all-gather(bf16[2,128,128]{2,1,0:T(8,128)(2,1)} %param.19), channel_id=1, replica_groups=mesh['chip'=8,'core'=2,'blk'=8,'samp'=2] {'samp'}, dimensions={2}, use_global_device_ids=true | all-gather | bytes 196608 | tf_op jit(solution)/shard_map/all_gather | solution.py:298
  59.6 0.7 pad_maximum_fusion
  61.0 3.4 %all-to-all-start.1 = ((f32[8,3,8,128]{3,2,1,0:T(8,128)}), f32[8,3,8,128]{3,2,1,0:T(8,128)S(1)}, u32[]{:S(2)}, u32[]{:S(2)}) async-start(f32[8,3,8,128]{3,2,1,0:T(8,128)} %broadcast_in_dim.11), calls=%async_computation.1 | async-start | bytes 196608 | tf_op jit(solution)/shard_map/all_to_all | solution.py:27
  65.7 8.3 %all-to-all-done.1 = f32[8,3,8,128]{3,2,1,0:T(8,128)S(1)} async-done(((f32[8,3,8,128]{3,2,1,0:T(8,128)}), f32[8,3,8,128]{3,2,1,0:T(8,128)S(1)}, u32[]{:S(2)}, u32[]{:S(2)}) %all-to-all-start.1) | async-done | bytes 98336 | tf_op jit(solution)/shard_map/all_to_all | solution.py:27
  74.1 4.6 %all-gather.5.cloned.1.call-done = bf16[32,128,1024]{2,1,0:T(8,128)(2,1)} async-done(((bf16[2,128,1024]{2,1,0:T(8,128)(2,1)}), bf16[32,128,1024]{2,1,0:T(8,128)(2,1)}) %all-gather.5.cloned.1.call-update) | async-done | bytes 8388624 | tf_op jit(solution)/shard_map/all_gather | solution.py:282
  78.6 4.3 %forward_first.1 = (bf16[4,8,128,1024]{3,2,1,0:T(8,128)(2,1)S(1)}, f32[4,8,1024]{2,1,0:T(8,128)S(1)}, f32[8,1024]{1,0:T(8,128)S(1)}) custom-call(f32[8,1024]{1,0:T(8,128)S(1)} %slice_bitcast_fusion.state_ref, f32[2,8,1024]{2,1,0:T(8,128)S(1)} %copy_bitcast_fusion.near_in, f32[2,8,1024]{2,1,0:T(8,128)S(1)} %collective-permute-done.2.far_in, ...), custom_call_target="tpu_custom_call" | custom-call | tf_op jit(solution)/shard_map/forward_first/pallas_call | solution.py:317
  83.0 2.6 %collective-permute-start.3 = (f32[8,1024]{1,0:T(8,128)S(1)}, f32[8,1024]{1,0:T(8,128)S(1)}, u32[]{:S(2)}, u32[]{:S(2)}) collective-permute-start(f32[8,1024]{1,0:T(8,128)S(1)} %get-tuple-element.47), channel_id=1, source_target_pairs={{0,32},{1,33},{2,34},{3,35},{4,36},{5,37},{6,38},{7,39},{8,40},{9,... | collective-permute-start | bytes 98312 | tf_op jit(solution)/shard_map/ppermute | solution.py:322
  85.5 2.5 %flip_trans.1.mats = bf16[4,1024,1024]{2,1,0:T(8,128)(2,1)S(1)} custom-call(bf16[4,8,128,1024]{3,2,1,0:T(8,128)(2,1)S(1)} %get-tuple-element.48.mats_ref), custom_call_target="tpu_custom_call" | custom-call | tf_op jit(solution)/shard_map/flip_trans/pallas_call | solution.py:287
  93.1 0.9 predict.1.pred_ref
  94.0 40.9 %all-gather.7.cloned.1.call-done = bf16[32,128,1024]{2,1,0:T(8,128)(2,1)} async-done(((bf16[2,128,1024]{2,1,0:T(8,128)(2,1)}), bf16[32,128,1024]{2,1,0:T(8,128)(2,1)}) %all-gather.7.cloned.1.call-update) | async-done | bytes 8388624 | tf_op jit(solution)/shard_map/all_gather | solution.py:282
  135.0 3.5 %backward_first.1 = (bf16[4,8,128,1024]{3,2,1,0:T(8,128)(2,1)S(1)}, f32[4,8,1024]{2,1,0:T(8,128)S(1)}, f32[8,1024]{1,0:T(8,128)S(1)}) custom-call(f32[4,8,1024]{2,1,0:T(8,128)S(1)} %get-tuple-element.62.filt_ref, f32[4,8,1024]{2,1,0:T(8,128)S(1)} %predict.1.pred_ref, bf16[2,8,2,128,1024]{4,3,2,1,0:T(8,128)(2,1)} %bitcast.25), custom_call_target="tpu_custom_call" | custom-call | tf_op jit(solution)/shard_map/backward_first/pallas_call | solution.py:330
  139.2 2.5 %flip_smooth.1.mats = bf16[4,1024,1024]{2,1,0:T(8,128)(2,1)S(1)} custom-call(bf16[4,8,128,1024]{3,2,1,0:T(8,128)(2,1)S(1)} %get-tuple-element.68.mats_ref), custom_call_target="tpu_custom_call" | custom-call | tf_op jit(solution)/shard_map/flip_smooth/pallas_call | solution.py:287
  145.3 1.3 collective-permute-start.16
  146.6 32.5 %collective-permute-done.16.state_ref = f32[8,1024]{1,0:T(8,128)S(1)} collective-permute-done((f32[8,1024]{1,0:T(8,128)S(1)}, f32[8,1024]{1,0:T(8,128)S(1)}, u32[]{:S(2)}, u32[]{:S(2)}) %collective-permute-start.16) | collective-permute-done | bytes 32800 | tf_op jit(solution)/shard_map/ppermute | solution.py:335
  179.1 1.9 %backward.13 = (f32[4,8,1024]{2,1,0:T(8,128)S(1)}, f32[8,1024]{1,0:T(8,128)}) custom-call(f32[8,1024]{1,0:T(8,128)S(1)} %collective-permute-done.16.state_ref, f32[4,8,1024]{2,1,0:T(8,128)S(1)} %get-tuple-element.62.filt_ref, f32[4,8,1024]{2,1,0:T(8,128)S(1)} %predict.1.pred_ref, ...), custom_call_target="tpu_custom_call", output_to_operand_aliasing={{0}: (4, {})} | custom-call | tf_op jit(solution)/shard_map/backward/pallas_call | solution.py:337
  (74 shorter events, 15.5 us)
Async XLA Ops:
  6.5 72.1 %all-gather.5.cloned.1.call-start = ((), (), s32[]{:S(2)}) async-start(), calls=%async_computation.2 | async-start | bytes 8912896 | tf_op jit(solution)/shard_map/all_gather | solution.py:282
  17.1 117.9 %all-gather.7.cloned.1.call-start = ((), (), s32[]{:S(2)}) async-start(), calls=%async_computation.3 | async-start | bytes 8912896 | tf_op jit(solution)/shard_map/all_gather | solution.py:282
  18.0 9.7 %collective-permute-start = (f32[2,8,16]{2,1,0:T(8,128)S(1)}, f32[2,8,16]{2,1,0:T(8,128)S(1)}, u32[]{:S(2)}, u32[]{:S(2)}) collective-permute-start(f32[2,8,16]{2,1,0:T(8,128)S(1)} %get-tuple-element.83), channel_id=1, source_target_pairs={{0,2},{2,4},{4,6},{6,8},{8,10},{10,12},{12,14},{14,0},{1,3},{3,5},... | collective-permute-start | bytes 3080 | tf_op jit(solution)/shard_map/ppermute | solution.py:32
  19.9 7.8 %collective-permute-start.1 = (f32[2,8,16]{2,1,0:T(8,128)S(1)}, f32[2,8,16]{2,1,0:T(8,128)S(1)}, u32[]{:S(2)}, u32[]{:S(2)}) collective-permute-start(f32[2,8,16]{2,1,0:T(8,128)S(1)} %get-tuple-element.84), channel_id=1, source_target_pairs={{0,14},{2,0},{4,2},{6,4},{8,6},{10,8},{12,10},{14,12},{1,15},{3,1}... | collective-permute-start | bytes 3080 | tf_op jit(solution)/shard_map/ppermute | solution.py:33
  61.0 13.1 %all-to-all-start.1 = ((f32[8,3,8,128]{3,2,1,0:T(8,128)}), f32[8,3,8,128]{3,2,1,0:T(8,128)S(1)}, u32[]{:S(2)}, u32[]{:S(2)}) async-start(f32[8,3,8,128]{3,2,1,0:T(8,128)} %broadcast_in_dim.11), calls=%async_computation.1 | async-start | bytes 196608 | tf_op jit(solution)/shard_map/all_to_all | solution.py:27
  64.3 0.7 copy-start.1
  74.0 4.6 %collective-permute-start.2 = (f32[2,8,1024]{2,1,0:T(8,128)S(1)}, f32[2,8,1024]{2,1,0:T(8,128)S(1)}, u32[]{:S(2)}, u32[]{:S(2)}) collective-permute-start(f32[2,8,1024]{2,1,0:T(8,128)S(1)} %copy_bitcast_fusion.near_in), channel_id=1, source_target_pairs={{0,16},{16,0},{1,17},{17,1},{2,18},{18,2},{3,19},{19,3},{4,20},{20... | collective-permute-start | bytes 196616 | tf_op jit(solution)/shard_map/ppermute | solution.py:303
  83.0 5.1 %collective-permute-start.3 = (f32[8,1024]{1,0:T(8,128)S(1)}, f32[8,1024]{1,0:T(8,128)S(1)}, u32[]{:S(2)}, u32[]{:S(2)}) collective-permute-start(f32[8,1024]{1,0:T(8,128)S(1)} %get-tuple-element.47), channel_id=1, source_target_pairs={{0,32},{1,33},{2,34},{3,35},{4,36},{5,37},{6,38},{7,39},{8,40},{9,... | collective-permute-start | bytes 98312 | tf_op jit(solution)/shard_map/ppermute | solution.py:322
  88.1 0.7 collective-permute-start.4
  88.8 0.7 collective-permute-start.5
  89.5 0.7 collective-permute-start.6
  90.2 0.7 collective-permute-start.7
  90.9 0.7 collective-permute-start.8
  91.8 0.7 collective-permute-start.9
  138.5 3.2 %collective-permute-start.10 = (f32[8,1024]{1,0:T(8,128)S(1)}, f32[8,1024]{1,0:T(8,128)S(1)}, u32[]{:S(2)}, u32[]{:S(2)}) collective-permute-start(f32[8,1024]{1,0:T(8,128)S(1)} %get-tuple-element.67), channel_id=1, source_target_pairs={{224,192},{225,193},{226,194},{227,195},{228,196},{229,197},{230,1... | collective-permute-start | bytes 98312 | tf_op jit(solution)/shard_map/ppermute | solution.py:335
  141.7 0.7 collective-permute-start.11
  142.4 0.7 collective-permute-start.12
  143.1 0.7 collective-permute-start.13
  143.8 0.7 collective-permute-start.14
  144.5 0.7 collective-permute-start.15
  145.2 35.8 %copy-start = (f32[2,8,128]{2,1,0:T(8,128)S(1)}, f32[2,8,128]{2,1,0:T(8,128)}, u32[]{:S(2)}) copy-start(f32[2,8,128]{2,1,0:T(8,128)} %prior_ref.1) | copy-start | bytes 24580
  145.3 33.8 %collective-permute-start.16 = (f32[8,1024]{1,0:T(8,128)S(1)}, f32[8,1024]{1,0:T(8,128)S(1)}, u32[]{:S(2)}, u32[]{:S(2)}) collective-permute-start(f32[8,1024]{1,0:T(8,128)S(1)} %get-tuple-element.80), channel_id=1, source_target_pairs={{32,0},{33,1},{34,2},{35,3},{36,4},{37,5},{38,6},{39,7},{40,8},{41... | collective-permute-start | bytes 98312 | tf_op jit(solution)/shard_map/ppermute | solution.py:335
Sparse Core Ops, SparseCore 0:
  17.2 61.3 all-gather.4
  80.5 54.4 all-gather.6

commit v5 on v4

--- a/solution.py
+++ b/solution.py
@@ -9,7 +9,7 @@
 highest = lax.Precision.HIGHEST
 bf16, f32 = jnp.bfloat16, jnp.float32
 ROWS_BY_ROWS = (((1,), (1,)), ((), ()))
-VMEM_LIMIT = 2 * 1024 * 1024
+VMEM_LIMIT = 12 * 1024 * 1024
 CHUNK = 256
 
 
@@ -107,17 +107,28 @@
     ]
 
 
+def flip_step(mats_ref, turn, out_ref):
+    rows = mats_ref.shape[2]
+    for k in range(0, mats_ref.shape[1], 2):
+        block = jnp.concatenate([mats_ref[turn, k], mats_ref[turn, k + 1]], axis=0)
+        for j in range(0, block.shape[1], 256):
+            out_ref[turn, j : j + 256, k * rows : (k + 2) * rows] = block[:, j : j + 256].T
+
+
 def flip_kernel(mats_ref, out_ref):
-    rows = mats_ref.shape[2]
-
     def step(turn, carry):
-        for k in range(0, mats_ref.shape[1], 2):
-            block = jnp.concatenate([mats_ref[turn, k], mats_ref[turn, k + 1]], axis=0)
-            for j in range(0, block.shape[1], 256):
-                out_ref[turn, j : j + 256, k * rows : (k + 2) * rows] = block[:, j : j + 256].T
+        flip_step(mats_ref, turn, out_ref)
         return carry
 
     lax.fori_loop(0, mats_ref.shape[0], step, 0)
+
+
+def pack_flip_kernel(rows_ref, sent_ref, out_ref, mats_ref, sems):
+    copies = start_pack(rows_ref, mats_ref, sems, range(4))
+    for turn in range(4):
+        for copy in copies[turn]:
+            copy.wait()
+        flip_step(mats_ref, turn, out_ref)
 
 
 def forward_step(apply, mats, turn, near_in, far_in, filt_ref, sent_ref):
@@ -145,7 +156,7 @@
             forward_step(apply_rows, mats_ref, at, near_in, far_in, filt_ref, sent_ref)
 
 
-def forward_kernel(hop, state_ref, near_in, far_in, mats, held_ref, filt_ref, sent_ref):
+def forward_kernel(hop, state_ref, near_in, far_in, mats, held_ref, filt_ref, sent_ref=None):
     @pl.when(lax.axis_index("chip") == hop)
     def _():
         chunks = in_chunks(state_ref)
@@ -157,7 +168,7 @@
                 inputs = (near_in[turn % 2, :, columns], far_in[turn % 2, :, columns])
                 state[n] = parts[n] + jnp.where(first, *(inputs if turn < 2 else inputs[::-1]))
                 filt_ref[turn, :, columns] = state[n]
-                if turn == 3:
+                if turn == 3 and sent_ref is not None:
                     sent_ref[:, columns] = state[n]
 
 
@@ -169,24 +180,20 @@
     sent_ref[...] = out_ref[turn]
 
 
-def backward_first_kernel(filt_ref, pred_ref, rows_ref, mats_ref, out_ref, sent_ref, sems):
-    copies = start_pack(rows_ref, mats_ref, sems, (2, 1, 0, 3))
-    out_ref[3] = filt_ref[3]
-    sent_ref[...] = filt_ref[3]
-    for turn in (2, 1, 0):
-        for copy in copies[turn]:
-            copy.wait()
-
-        @pl.when(lax.axis_index("chip") == lax.axis_size("chip") - 1)
-        def _():
+def backward_first_kernel(filt_ref, pred_ref, rows_ref, out_ref, sent_ref, mats_ref, sems):
+    @pl.when(lax.axis_index("chip") == lax.axis_size("chip") - 1)
+    def _():
+        copies = start_pack(rows_ref, mats_ref, sems, (2, 1, 0))
+        out_ref[3] = filt_ref[3]
+        sent_ref[...] = filt_ref[3]
+        for turn in (2, 1, 0):
+            for copy in copies[turn]:
+                copy.wait()
             at = jnp.int32(turn)
             backward_step(apply_rows, mats_ref, at, filt_ref, pred_ref, out_ref, sent_ref)
 
-    for copy in copies[3]:
-        copy.wait()
-
-
-def backward_kernel(hop, state_ref, filt_ref, pred_ref, mats, held_ref, out_ref, sent_ref):
+
+def backward_kernel(hop, state_ref, filt_ref, pred_ref, mats, held_ref, out_ref, sent_ref=None):
     @pl.when(lax.axis_index("chip") == hop)
     def _():
         chunks = in_chunks(state_ref)
@@ -197,7 +204,7 @@
             for n, columns in enumerate(chunks):
                 state[n] = filt_ref[turn, :, columns] + parts[n]
                 out_ref[turn, :, columns] = state[n]
-                if turn == 0:
+                if turn == 0 and sent_ref is not None:
                     sent_ref[:, columns] = state[n]
 
 
@@ -314,27 +321,34 @@
     kron, start = lax.optimization_barrier((kron, start))
     dmas = [pltpu.SemaphoreType.DMA((4, 4))]
     shapes = (mats_shape, filt_shape, state_shape)
-    trans, filtered, sent = call(
+    trans, filtered, *sent = call(
         forward_first_kernel, "forward_first", shapes, [VMEM] * 3 + [HBM], dmas
     )(start, near_in, far_in, in_hbm(trans_rows))
     trans = flip(in_vmem(trans), "flip_trans")
     for hop in range(1, groups):
-        state = lax.ppermute(sent, "chip", [(hop - 1, hop)])
+        state = lax.ppermute(sent[0], "chip", [(hop - 1, hop)])
         kernel = functools.partial(forward_kernel, hop)
-        filtered, sent = call(kernel, "forward", shapes[1:], [VMEM] * 5, (), {4: 0})(
+        made = shapes[1:] if hop < groups - 1 else shapes[1:2]
+        filtered, *sent = call(kernel, "forward", made, [VMEM] * 5, (), {4: 0})(
             state, near_in, far_in, trans, filtered
         )
 
     predicted = call(predict_kernel, "predict", filt_shape, [VMEM, VMEM])(kron, filtered)
     smooth_rows, predicted = lax.optimization_barrier((smooth_rows, predicted))
-    smooth, smoothed, sent = call(
-        backward_first_kernel, "backward_first", shapes, [VMEM] * 2 + [HBM], dmas
+    held = pltpu.VMEM(mats_shape.shape, bf16)
+    smoothed, *sent = call(
+        backward_first_kernel, "backward_first", shapes[1:], [VMEM] * 2 + [HBM], [held] + dmas
     )(filtered, predicted, in_hbm(smooth_rows))
-    smooth = flip(in_vmem(smooth), "flip_smooth")
+    flipped = jax.ShapeDtypeStruct((4, state_count, state_count), bf16)
+    smooth = call(pack_flip_kernel, "pack_flip", flipped, [HBM, VMEM], [held] + dmas)(
+        in_hbm(smooth_rows), sent[0]
+    )
+    smooth = in_vmem(smooth)
     for hop in range(groups - 2, -1, -1):
-        state = lax.ppermute(sent, "chip", [(hop + 1, hop)])
+        state = lax.ppermute(sent[0], "chip", [(hop + 1, hop)])
         kernel = functools.partial(backward_kernel, hop)
-        smoothed, sent = call(kernel, "backward", shapes[1:], [VMEM] * 5, (), {4: 0})(
+        made = shapes[1:] if hop > 0 else shapes[1:2]
+        smoothed, *sent = call(kernel, "backward", made, [VMEM] * 5, (), {4: 0})(
             state, filtered, predicted, smooth, smoothed
         )
     out_shape = jax.ShapeDtypeStruct(prior_path.shape, f32)

time: 189 us -> 187 us (0.989)
  Pallas kernels: 18 us -> 15.1 us
    pallas_call x2 -> x1, Pallas kernels: 5.05 us -> 2.53 us  [flip(): return in_vmem(call(flip_kernel, name, shape, [VMEM])(mats))]
    pallas_call x15 -> x16, Pallas kernels: 6.42 us -> 6.04 us  [the longest x1 4.22 us: on_device(): call(pack_flip_kernel, 'pack_flip', flipped, [HBM, VMEM], [held] + dmas)]
  transfers between devices with their start and end apart: 20 -> 20, of which waited for: 4 -> 4; matrix products, arithmetic and copies ran while one was open for 5% -> 5% of each run, Pallas kernels for 6% -> 7%
where the time goes in v5:
time: 187 us; the launch traced here: 186 us
  waiting for transfers between devices  87.4 us (47%)
  blocking collectives  39.8 us (21%)
  starting transfers between devices  21.1 us (11%)
  Pallas kernels  15.1 us (8%)
  between operations  13.9 us (7%)
  local copies, waits for them, and re-layouts  5.1 us (3%)
  other arithmetic  3.03 us (2%)
    all_gather x2, waiting for transfers between devices, all_rows(): rows = lax.all_gather(whole, ('core', 'blk'), axis=0)  46.1 us
    ppermute x7, waiting for transfers between devices, on_device(): state = lax.ppermute(sent[0], 'chip', [(hop + 1, hop)])  32.9 us
    all_gather x2, blocking collectives, all_rows(): whole = lax.all_gather(mats, 'samp', axis=2, tiled=True)  19.5 us
    all_to_all x1, blocking collectives, all_blocks(): return lax.all_to_all(copies, axis, 0, 0, tiled=True)  13.6 us
    all_to_all x1, waiting for transfers between devices, all_blocks(): return lax.all_to_all(copies, axis, 0, 0, tiled=True)  8.32 us
    all_gather x1, blocking collectives, on_device(): gain = lax.all_gather(gain_mats, 'samp', axis=2, tiled=True)  6.68 us
    ppermute x7, starting transfers between devices, on_device(): state = lax.ppermute(sent[0], 'chip', [(hop - 1, hop)])  6.55 us
    ppermute x7, starting transfers between devices, on_device(): state = lax.ppermute(sent[0], 'chip', [(hop + 1, hop)])  5.27 us
  transfers between devices with their start and end apart: 20, of which 4 were waited for; matrix products, arithmetic and copies ran while one was open for 5% of the time, Pallas kernels for 7%

profile of v5, /device:TPU:16, one launch (start us, length us, event | category | flops | bytes accessed | tf_op | source)
XLA Modules:
  0.0 186.5 jit_solution(12248037667580532883)
XLA Ops:
  6.5 10.5 %all_gather.22 = bf16[2,128,1024]{2,1,0:T(8,128)(2,1)} all-gather(bf16[2,128,512]{2,1,0:T(8,128)(2,1)} %param.18), channel_id=1, replica_groups=mesh['chip'=8,'core'=2,'blk'=8,'samp'=2] {'samp'}, dimensions={2}, use_global_device_ids=true | all-gather | bytes 786432 | tf_op jit(solution)/shard_map/all_gather | solution.py:288
  17.1 0.8 fusion.10
  18.0 1.9 %collective-permute-start = (f32[2,8,16]{2,1,0:T(8,128)S(1)}, f32[2,8,16]{2,1,0:T(8,128)S(1)}, u32[]{:S(2)}, u32[]{:S(2)}) collective-permute-start(f32[2,8,16]{2,1,0:T(8,128)S(1)} %get-tuple-element.77), channel_id=1, source_target_pairs={{0,2},{2,4},{4,6},{6,8},{8,10},{10,12},{12,14},{14,0},{1,3},{3,5},... | collective-permute-start | bytes 3080 | tf_op jit(solution)/shard_map/ppermute | solution.py:32
  19.9 4.0 %collective-permute-start.1 = (f32[2,8,16]{2,1,0:T(8,128)S(1)}, f32[2,8,16]{2,1,0:T(8,128)S(1)}, u32[]{:S(2)}, u32[]{:S(2)}) collective-permute-start(f32[2,8,16]{2,1,0:T(8,128)S(1)} %get-tuple-element.78), channel_id=1, source_target_pairs={{0,14},{2,0},{4,2},{6,4},{8,6},{10,8},{12,10},{14,12},{1,15},{3,1}... | collective-permute-start | bytes 3080 | tf_op jit(solution)/shard_map/ppermute | solution.py:33
  23.9 0.8 copy.42
  25.9 0.8 copy.40
  26.8 0.7 convert_element_type.10
  27.7 0.9 fusion
  28.7 13.6 %all_to_all.10 = f32[8,1,512]{2,1,0:T(1,128)S(1)} all-to-all(f32[8,1,512]{2,1,0:T(1,128)S(1)} %reshape.49), channel_id=1, replica_groups=mesh['chip'=8,'core'=2,'blk'=8,'samp'=2] {'blk'}, dimensions={0} | all-to-all | bytes 32768 | tf_op jit(solution)/shard_map/all_to_all | solution.py:27
  43.7 9.0 %all_gather.25 = bf16[2,128,1024]{2,1,0:T(8,128)(2,1)} all-gather(bf16[2,128,512]{2,1,0:T(8,128)(2,1)} %param.20), channel_id=1, replica_groups=mesh['chip'=8,'core'=2,'blk'=8,'samp'=2] {'samp'}, dimensions={2}, use_global_device_ids=true | all-gather | bytes 786432 | tf_op jit(solution)/shard_map/all_gather | solution.py:288
  52.7 6.7 %all_gather.21 = bf16[2,128,256]{2,1,0:T(8,128)(2,1)S(1)} all-gather(bf16[2,128,128]{2,1,0:T(8,128)(2,1)} %param.19), channel_id=1, replica_groups=mesh['chip'=8,'core'=2,'blk'=8,'samp'=2] {'samp'}, dimensions={2}, use_global_device_ids=true | all-gather | bytes 196608 | tf_op jit(solution)/shard_map/all_gather | solution.py:305
  59.6 0.7 pad_maximum_fusion
  61.0 3.4 %all-to-all-start.1 = ((f32[8,3,8,128]{3,2,1,0:T(8,128)}), f32[8,3,8,128]{3,2,1,0:T(8,128)S(1)}, u32[]{:S(2)}, u32[]{:S(2)}) async-start(f32[8,3,8,128]{3,2,1,0:T(8,128)} %broadcast_in_dim.11), calls=%async_computation.1 | async-start | bytes 196608 | tf_op jit(solution)/shard_map/all_to_all | solution.py:27
  65.7 8.3 %all-to-all-done.1 = f32[8,3,8,128]{3,2,1,0:T(8,128)S(1)} async-done(((f32[8,3,8,128]{3,2,1,0:T(8,128)}), f32[8,3,8,128]{3,2,1,0:T(8,128)S(1)}, u32[]{:S(2)}, u32[]{:S(2)}) %all-to-all-start.1) | async-done | bytes 98336 | tf_op jit(solution)/shard_map/all_to_all | solution.py:27
  74.0 4.6 %all-gather.5.cloned.1.call-done = bf16[32,128,1024]{2,1,0:T(8,128)(2,1)} async-done(((bf16[2,128,1024]{2,1,0:T(8,128)(2,1)}), bf16[32,128,1024]{2,1,0:T(8,128)(2,1)}) %all-gather.5.cloned.1.call-update) | async-done | bytes 8388624 | tf_op jit(solution)/shard_map/all_gather | solution.py:289
  78.6 4.3 %forward_first.1 = (bf16[4,8,128,1024]{3,2,1,0:T(8,128)(2,1)S(1)}, f32[4,8,1024]{2,1,0:T(8,128)S(1)}, f32[8,1024]{1,0:T(8,128)S(1)}) custom-call(f32[8,1024]{1,0:T(8,128)S(1)} %slice_bitcast_fusion.state_ref, f32[2,8,1024]{2,1,0:T(8,128)S(1)} %copy_bitcast_fusion.near_in, f32[2,8,1024]{2,1,0:T(8,128)S(1)} %collective-permute-done.2.far_in, ...), custom_call_target="tpu_custom_call" | custom-call | tf_op jit(solution)/shard_map/forward_first/pallas_call | solution.py:324
  82.9 2.6 %collective-permute-start.3 = (f32[8,1024]{1,0:T(8,128)S(1)}, f32[8,1024]{1,0:T(8,128)S(1)}, u32[]{:S(2)}, u32[]{:S(2)}) collective-permute-start(f32[8,1024]{1,0:T(8,128)S(1)} %get-tuple-element.44), channel_id=1, source_target_pairs={{0,32},{1,33},{2,34},{3,35},{4,36},{5,37},{6,38},{7,39},{8,40},{9,... | collective-permute-start | bytes 98312 | tf_op jit(solution)/shard_map/ppermute | solution.py:329
  85.5 2.5 %flip_trans.1.mats = bf16[4,1024,1024]{2,1,0:T(8,128)(2,1)S(1)} custom-call(bf16[4,8,128,1024]{3,2,1,0:T(8,128)(2,1)S(1)} %get-tuple-element.45.mats_ref), custom_call_target="tpu_custom_call" | custom-call | tf_op jit(solution)/shard_map/flip_trans/pallas_call | solution.py:294
  92.5 0.9 predict.1.pred_ref
  93.4 41.5 %all-gather.7.cloned.1.call-done = bf16[32,128,1024]{2,1,0:T(8,128)(2,1)} async-done(((bf16[2,128,1024]{2,1,0:T(8,128)(2,1)}), bf16[32,128,1024]{2,1,0:T(8,128)(2,1)}) %all-gather.7.cloned.1.call-update) | async-done | bytes 8388624 | tf_op jit(solution)/shard_map/all_gather | solution.py:289
  135.8 4.2 %pack_flip.1.mats = bf16[4,1024,1024]{2,1,0:T(8,128)(2,1)S(1)} custom-call(bf16[2,8,2,128,1024]{4,3,2,1,0:T(8,128)(2,1)} %bitcast.26, f32[8,1024]{1,0:T(8,128)S(1)} %get-tuple-element.63.sent_ref), custom_call_target="tpu_custom_call" | custom-call | tf_op jit(solution)/shard_map/pack_flip/pallas_call | solution.py:343
  143.6 1.3 collective-permute-start.16
  144.9 32.9 %collective-permute-done.16.state_ref = f32[8,1024]{1,0:T(8,128)S(1)} collective-permute-done((f32[8,1024]{1,0:T(8,128)S(1)}, f32[8,1024]{1,0:T(8,128)S(1)}, u32[]{:S(2)}, u32[]{:S(2)}) %collective-permute-start.16) | collective-permute-done | bytes 32800 | tf_op jit(solution)/shard_map/ppermute | solution.py:348
  177.8 1.3 backward.13.smooth_ref
  (74 shorter events, 14.3 us)
Async XLA Ops:
  6.5 72.1 %all-gather.5.cloned.1.call-start = ((), (), s32[]{:S(2)}) async-start(), calls=%async_computation.2 | async-start | bytes 8912896 | tf_op jit(solution)/shard_map/all_gather | solution.py:289
  17.1 117.8 %all-gather.7.cloned.1.call-start = ((), (), s32[]{:S(2)}) async-start(), calls=%async_computation.3 | async-start | bytes 8912896 | tf_op jit(solution)/shard_map/all_gather | solution.py:289
  18.0 9.7 %collective-permute-start = (f32[2,8,16]{2,1,0:T(8,128)S(1)}, f32[2,8,16]{2,1,0:T(8,128)S(1)}, u32[]{:S(2)}, u32[]{:S(2)}) collective-permute-start(f32[2,8,16]{2,1,0:T(8,128)S(1)} %get-tuple-element.77), channel_id=1, source_target_pairs={{0,2},{2,4},{4,6},{6,8},{8,10},{10,12},{12,14},{14,0},{1,3},{3,5},... | collective-permute-start | bytes 3080 | tf_op jit(solution)/shard_map/ppermute | solution.py:32
  19.9 7.8 %collective-permute-start.1 = (f32[2,8,16]{2,1,0:T(8,128)S(1)}, f32[2,8,16]{2,1,0:T(8,128)S(1)}, u32[]{:S(2)}, u32[]{:S(2)}) collective-permute-start(f32[2,8,16]{2,1,0:T(8,128)S(1)} %get-tuple-element.78), channel_id=1, source_target_pairs={{0,14},{2,0},{4,2},{6,4},{8,6},{10,8},{12,10},{14,12},{1,15},{3,1}... | collective-permute-start | bytes 3080 | tf_op jit(solution)/shard_map/ppermute | solution.py:33
  61.0 13.1 %all-to-all-start.1 = ((f32[8,3,8,128]{3,2,1,0:T(8,128)}), f32[8,3,8,128]{3,2,1,0:T(8,128)S(1)}, u32[]{:S(2)}, u32[]{:S(2)}) async-start(f32[8,3,8,128]{3,2,1,0:T(8,128)} %broadcast_in_dim.11), calls=%async_computation.1 | async-start | bytes 196608 | tf_op jit(solution)/shard_map/all_to_all | solution.py:27
  64.3 0.7 copy-start.1
  74.0 4.6 %collective-permute-start.2 = (f32[2,8,1024]{2,1,0:T(8,128)S(1)}, f32[2,8,1024]{2,1,0:T(8,128)S(1)}, u32[]{:S(2)}, u32[]{:S(2)}) collective-permute-start(f32[2,8,1024]{2,1,0:T(8,128)S(1)} %copy_bitcast_fusion.near_in), channel_id=1, source_target_pairs={{0,16},{16,0},{1,17},{17,1},{2,18},{18,2},{3,19},{19,3},{4,20},{20... | collective-permute-start | bytes 196616 | tf_op jit(solution)/shard_map/ppermute | solution.py:310
  82.9 5.1 %collective-permute-start.3 = (f32[8,1024]{1,0:T(8,128)S(1)}, f32[8,1024]{1,0:T(8,128)S(1)}, u32[]{:S(2)}, u32[]{:S(2)}) collective-permute-start(f32[8,1024]{1,0:T(8,128)S(1)} %get-tuple-element.44), channel_id=1, source_target_pairs={{0,32},{1,33},{2,34},{3,35},{4,36},{5,37},{6,38},{7,39},{8,40},{9,... | collective-permute-start | bytes 98312 | tf_op jit(solution)/shard_map/ppermute | solution.py:329
  88.1 0.7 collective-permute-start.4
  88.8 0.7 collective-permute-start.5
  89.5 0.7 collective-permute-start.6
  90.2 0.7 collective-permute-start.7
  90.9 0.7 collective-permute-start.8
  91.8 0.7 collective-permute-start.9
  135.1 4.9 %collective-permute-start.10 = (f32[8,1024]{1,0:T(8,128)S(1)}, f32[8,1024]{1,0:T(8,128)S(1)}, u32[]{:S(2)}, u32[]{:S(2)}) collective-permute-start(f32[8,1024]{1,0:T(8,128)S(1)} %get-tuple-element.63.sent_ref), channel_id=1, source_target_pairs={{224,192},{225,193},{226,194},{227,195},{228,196},{229,197},{230,1... | collective-permute-start | bytes 98312 | tf_op jit(solution)/shard_map/ppermute | solution.py:348
  140.0 0.7 collective-permute-start.11
  140.7 0.7 collective-permute-start.12
  141.4 0.7 collective-permute-start.13
  142.1 0.7 collective-permute-start.14
  142.8 0.7 collective-permute-start.15
  143.5 35.5 %copy-start = (f32[2,8,128]{2,1,0:T(8,128)S(1)}, f32[2,8,128]{2,1,0:T(8,128)}, u32[]{:S(2)}) copy-start(f32[2,8,128]{2,1,0:T(8,128)} %prior_ref.1) | copy-start | bytes 24580
  143.6 34.2 %collective-permute-start.16 = (f32[8,1024]{1,0:T(8,128)S(1)}, f32[8,1024]{1,0:T(8,128)S(1)}, u32[]{:S(2)}, u32[]{:S(2)}) collective-permute-start(f32[8,1024]{1,0:T(8,128)S(1)} %get-tuple-element.75), channel_id=1, source_target_pairs={{32,0},{33,1},{34,2},{35,3},{36,4},{37,5},{38,6},{39,7},{40,8},{41... | collective-permute-start | bytes 98312 | tf_op jit(solution)/shard_map/ppermute | solution.py:348
Sparse Core Ops, SparseCore 0:
  17.2 61.3 all-gather.4
  80.4 54.4 all-gather.6

commit v6 on v5

--- a/solution.py
+++ b/solution.py
@@ -11,6 +11,7 @@
 ROWS_BY_ROWS = (((1,), (1,)), ((), ()))
 VMEM_LIMIT = 12 * 1024 * 1024
 CHUNK = 256
+RING_ROWS = 32
 
 
 def ring(count, step):
@@ -72,7 +73,7 @@
             blocks = pl.ds(part * size, size)
             copy = pltpu.make_async_copy(
                 rows_ref.at[turn // steps, blocks, turn % steps],
-                mats_ref.at[turn, blocks],
+                mats_ref.at[turn, blocks, pl.ds(0, rows_ref.shape[3])],
                 sems.at[turn, part],
             )
             copy.start()
@@ -143,8 +144,21 @@
     sent_ref[...] = filt_ref[turn]
 
 
-def forward_first_kernel(state_ref, near_in, far_in, rows_ref, mats_ref, filt_ref, sent_ref, sems):
+def forward_first_kernel(state_ref, near_in, far_in, rows_ref, *refs):
+    shards, (mats_ref, filt_ref, sent_ref, sems, ring_sems) = refs[:-5], refs[-5:]
+    blk, core, count = lax.axis_index("blk"), lax.axis_index("core"), len(refs[:-5]) // 2
+    ring_copies = []
+    for n, shard in enumerate(shards):
+        steps, rows, _ = shard.shape
+        owner = core if n < count else 1 - core
+        at = lax.rem(blk - n % count + count, count)
+        place = pl.ds(rows_ref.shape[3], rows)
+        target = mats_ref.at[pl.ds(owner * steps, steps), at, place]
+        ring_copies.append(pltpu.make_async_copy(shard, target, ring_sems.at[n]))
+        ring_copies[-1].start()
     copies = start_pack(rows_ref, mats_ref, sems, range(4))
+    for copy in ring_copies:
+        copy.wait()
     sent_ref[...] = state_ref[...]
     for turn in range(4):
         for copy in copies[turn]:
@@ -241,6 +255,7 @@
 SMEM = pl.BlockSpec(memory_space=pltpu.SMEM)
 VMEM = pl.BlockSpec(memory_space=pltpu.VMEM)
 HBM = pl.BlockSpec(memory_space=pltpu.HBM)
+ANY = pl.BlockSpec(memory_space=pl.ANY)
 
 
 def call(kernel, name, shapes, specs, scratch=(), aliases=None):
@@ -284,8 +299,10 @@
 
     mats_shape = jax.ShapeDtypeStruct((4, cycle, trans_mats.shape[1], state_count), bf16)
 
-    def all_rows(mats):
-        whole = lax.all_gather(mats, "samp", axis=2, tiled=True)
+    def whole_rows(mats):
+        return lax.all_gather(mats, "samp", axis=2, tiled=True)
+
+    def all_rows(whole):
         rows = lax.all_gather(whole, ("core", "blk"), axis=0)
         return rows.reshape((2, cycle) + rows.shape[1:])
 
@@ -293,7 +310,16 @@
         shape = jax.ShapeDtypeStruct((4, state_count, state_count), bf16)
         return in_vmem(call(flip_kernel, name, shape, [VMEM])(mats))
 
-    trans_rows = all_rows(trans_mats)
+    whole = whole_rows(trans_mats)
+    cut = whole.shape[1] - RING_ROWS
+    trans_rows = all_rows(whole[:, :cut])
+    shards, back = [whole[:, cut:]], []
+    for k in range(cycle // 2):
+        shards.append(lax.ppermute(shards[-1], "blk", ring(cycle, 1)))
+        if k < cycle // 2 - 1:
+            back.append(lax.ppermute(back[-1] if back else shards[0], "blk", ring(cycle, -1)))
+    shards += back[::-1]
+    shards += [lax.ppermute(shard, "core", swapped(2)) for shard in shards]
 
     widened, mixer = noise_rim(noise_draw), noise_mixer(wend_blocks, block_cols)
     obs_noise = jnp.einsum("tsl,lm->tsm", widened, mixer, precision=highest)
@@ -311,7 +337,7 @@
     trans_rows, near_in = lax.optimization_barrier((trans_rows, near_in))
 
     smooth_mats, _ = lax.optimization_barrier((smooth_mats, all_resid))
-    smooth_rows = all_rows(smooth_mats)
+    smooth_rows = all_rows(whole_rows(smooth_mats))
 
     filt_shape = jax.ShapeDtypeStruct((4, sample_count, state_count), f32)
     state_shape = jax.ShapeDtypeStruct((sample_count, state_count), f32)
@@ -322,8 +348,12 @@
     dmas = [pltpu.SemaphoreType.DMA((4, 4))]
     shapes = (mats_shape, filt_shape, state_shape)
     trans, filtered, *sent = call(
-        forward_first_kernel, "forward_first", shapes, [VMEM] * 3 + [HBM], dmas
-    )(start, near_in, far_in, in_hbm(trans_rows))
+        forward_first_kernel,
+        "forward_first",
+        shapes,
+        [VMEM] * 3 + [HBM] + [ANY] * len(shards),
+        dmas + [pltpu.SemaphoreType.DMA((len(shards),))],
+    )(start, near_in, far_in, in_hbm(trans_rows), *shards)
     trans = flip(in_vmem(trans), "flip_trans")
     for hop in range(1, groups):
         state = lax.ppermute(sent[0], "chip", [(hop - 1, hop)])

time: 187 us -> 185 us (0.989)
  waiting for transfers between devices: 87.4 us -> 70.2 us
  starting transfers between devices: 21.1 us -> 33.9 us
    all_gather x2, waiting for transfers between devices: 46.1 us -> 28.8 us  [all_rows(): rows = lax.all_gather(whole, ('core', 'blk'), axis=0)]
    ppermute x0 -> x15, starting transfers between devices: none -> 12 us  [the longest x3 9.41 us: on_device(): lax.ppermute(back[-1] if back else shards[0], 'blk', ring(cycle, -1))]
    all_to_all x1, waiting for transfers between devices: 8.32 us -> 0.01 us  [all_blocks(): return lax.all_to_all(copies, axis, 0, 0, tiled=True)]
    ppermute x0 -> x15, waiting for transfers between devices: none -> 7.28 us  [the longest x4 4.2 us: on_device(): shards.append(lax.ppermute(shards[-1], 'blk', ring(cycle, 1)))]
  transfers between devices with their start and end apart: 20 -> 35, of which waited for: 4 -> 7; matrix products, arithmetic and copies ran while one was open for 5% -> 5% of each run, Pallas kernels for 7% -> 8%
where the time goes in v6:
time: 185 us; the launch traced here: 184 us
  waiting for transfers between devices  70.2 us (38%)
  blocking collectives  39.6 us (21%)
  starting transfers between devices  33.9 us (18%)
  Pallas kernels  16.4 us (9%)
  between operations  14 us (8%)
  local copies, waits for them, and re-layouts  5.9 us (3%)
  other arithmetic  3.01 us (2%)
    ppermute x7, waiting for transfers between devices, on_device(): state = lax.ppermute(sent[0], 'chip', [(hop + 1, hop)])  34.1 us
    all_gather x2, waiting for transfers between devices, all_rows(): rows = lax.all_gather(whole, ('core', 'blk'), axis=0)  28.8 us
    all_gather x2, blocking collectives, whole_rows(): return lax.all_gather(mats, 'samp', axis=2, tiled=True)  19.3 us
    all_to_all x1, blocking collectives, all_blocks(): return lax.all_to_all(copies, axis, 0, 0, tiled=True)  13.6 us
    ppermute x3, starting transfers between devices, on_device(): lax.ppermute(back[-1] if back else shards[0], 'blk', ring(cycle, -1))  9.41 us
    all_gather x1, blocking collectives, on_device(): gain = lax.all_gather(gain_mats, 'samp', axis=2, tiled=True)  6.67 us
    ppermute x7, starting transfers between devices, on_device(): state = lax.ppermute(sent[0], 'chip', [(hop - 1, hop)])  6.1 us
    pallas_call x1, Pallas kernels, on_device(): call(forward_first_kernel, 'forward_first', shapes, [VMEM] * 3 + [HBM] +...  5.81 us
  transfers between devices with their start and end apart: 35, of which 7 were waited for; matrix products, arithmetic and copies ran while one was open for 5% of the time, Pallas kernels for 8%

profile of v6, /device:TPU:16, one launch (start us, length us, event | category | flops | bytes accessed | tf_op | source)
XLA Modules:
  0.0 184.1 jit_solution(12026653426832132768)
XLA Ops:
  6.5 10.4 %all_gather.22 = bf16[2,128,1024]{2,1,0:T(8,128)(2,1)S(1)} all-gather(bf16[2,128,512]{2,1,0:T(8,128)(2,1)} %param.18), channel_id=1, replica_groups=mesh['chip'=8,'core'=2,'blk'=8,'samp'=2] {'samp'}, dimensions={2}, use_global_device_ids=true | all-gather | bytes 786432 | tf_op jit(solution)/shard_map/all_gather | solution.py:303
  17.8 0.8 fusion.10
  18.7 1.9 %collective-permute-start = (f32[2,8,16]{2,1,0:T(8,128)S(1)}, f32[2,8,16]{2,1,0:T(8,128)S(1)}, u32[]{:S(2)}, u32[]{:S(2)}) collective-permute-start(f32[2,8,16]{2,1,0:T(8,128)S(1)} %get-tuple-element.77), channel_id=1, source_target_pairs={{0,2},{2,4},{4,6},{6,8},{8,10},{10,12},{12,14},{14,0},{1,3},{3,5},... | collective-permute-start | bytes 3080 | tf_op jit(solution)/shard_map/ppermute | solution.py:33
  20.6 4.0 %collective-permute-start.1 = (f32[2,8,16]{2,1,0:T(8,128)S(1)}, f32[2,8,16]{2,1,0:T(8,128)S(1)}, u32[]{:S(2)}, u32[]{:S(2)}) collective-permute-start(f32[2,8,16]{2,1,0:T(8,128)S(1)} %get-tuple-element.78), channel_id=1, source_target_pairs={{0,14},{2,0},{4,2},{6,4},{8,6},{10,8},{12,10},{14,12},{1,15},{3,1}... | collective-permute-start | bytes 3080 | tf_op jit(solution)/shard_map/ppermute | solution.py:34
  28.4 0.9 fusion
  29.4 13.6 %all_to_all.10 = f32[8,1,512]{2,1,0:T(1,128)S(1)} all-to-all(f32[8,1,512]{2,1,0:T(1,128)S(1)} %reshape.49), channel_id=1, replica_groups=mesh['chip'=8,'core'=2,'blk'=8,'samp'=2] {'blk'}, dimensions={0} | all-to-all | bytes 32768 | tf_op jit(solution)/shard_map/all_to_all | solution.py:28
  44.4 8.9 %all_gather.25 = bf16[2,128,1024]{2,1,0:T(8,128)(2,1)} all-gather(bf16[2,128,512]{2,1,0:T(8,128)(2,1)} %param.20), channel_id=1, replica_groups=mesh['chip'=8,'core'=2,'blk'=8,'samp'=2] {'samp'}, dimensions={2}, use_global_device_ids=true | all-gather | bytes 786432 | tf_op jit(solution)/shard_map/all_gather | solution.py:303
  54.1 2.6 %collective-permute-start.7 = (bf16[2,32,1024]{2,1,0:T(8,128)(2,1)S(1)}, bf16[2,32,1024]{2,1,0:T(8,128)(2,1)S(1)}, u32[]{:S(2)}, u32[]{:S(2)}) collective-permute-start(bf16[2,32,1024]{2,1,0:T(8,128)(2,1)S(1)} %slice.37.refs_0_), channel_id=1, source_target_pairs={{0,14},{2,0},{4,2},{6,4},{8,6},{10,8},{12,10},{14,12},{1,15},{3,1}... | collective-permute-start | bytes 393224 | tf_op jit(solution)/shard_map/ppermute | solution.py:320
  56.7 6.7 %all_gather.21 = bf16[2,128,256]{2,1,0:T(8,128)(2,1)S(1)} all-gather(bf16[2,128,128]{2,1,0:T(8,128)(2,1)} %param.19), channel_id=1, replica_groups=mesh['chip'=8,'core'=2,'blk'=8,'samp'=2] {'samp'}, dimensions={2}, use_global_device_ids=true | all-gather | bytes 196608 | tf_op jit(solution)/shard_map/all_gather | solution.py:331
  64.9 4.5 %all-to-all-start.1 = ((f32[8,3,8,128]{3,2,1,0:T(8,128)}), f32[8,3,8,128]{3,2,1,0:T(8,128)S(1)}, u32[]{:S(2)}, u32[]{:S(2)}) async-start(f32[8,3,8,128]{3,2,1,0:T(8,128)} %broadcast_in_dim.11), calls=%async_computation.1 | async-start | bytes 196608 | tf_op jit(solution)/shard_map/all_to_all | solution.py:28
  69.4 3.2 %collective-permute-start.8 = (bf16[2,32,1024]{2,1,0:T(8,128)(2,1)S(1)}, bf16[2,32,1024]{2,1,0:T(8,128)(2,1)S(1)}, u32[]{:S(2)}, u32[]{:S(2)}) collective-permute-start(bf16[2,32,1024]{2,1,0:T(8,128)(2,1)S(1)} %collective-permute-done.7.refs_7_), channel_id=1, source_target_pairs={{0,14},{2,0},{4,2},{6,4},{8,6},{10,8},{12,10},{14,12},{1,15},{3,1}... | collective-permute-start | bytes 393224 | tf_op jit(solution)/shard_map/ppermute | solution.py:320
  73.6 1.8 collective-permute-done.8.refs_6_
  75.4 3.6 %collective-permute-start.9 = (bf16[2,32,1024]{2,1,0:T(8,128)(2,1)S(1)}, bf16[2,32,1024]{2,1,0:T(8,128)(2,1)S(1)}, u32[]{:S(2)}, u32[]{:S(2)}) collective-permute-start(bf16[2,32,1024]{2,1,0:T(8,128)(2,1)S(1)} %collective-permute-done.8.refs_6_), channel_id=1, source_target_pairs={{0,14},{2,0},{4,2},{6,4},{8,6},{10,8},{12,10},{14,12},{1,15},{3,1}... | collective-permute-start | bytes 393224 | tf_op jit(solution)/shard_map/ppermute | solution.py:320
  82.2 3.3 %collective-permute-done.6.refs_4_ = bf16[2,32,1024]{2,1,0:T(8,128)(2,1)S(1)} collective-permute-done((bf16[2,32,1024]{2,1,0:T(8,128)(2,1)S(1)}, bf16[2,32,1024]{2,1,0:T(8,128)(2,1)S(1)}, u32[]{:S(2)}, u32[]{:S(2)}) %collective-permute-start.6) | collective-permute-done | bytes 131104 | tf_op jit(solution)/shard_map/ppermute | solution.py:318
  85.6 1.3 collective-permute-done.14.refs_12_
  86.9 5.8 %forward_first.1 = (bf16[4,8,128,1024]{3,2,1,0:T(8,128)(2,1)S(1)}, f32[4,8,1024]{2,1,0:T(8,128)S(1)}, f32[8,1024]{1,0:T(8,128)S(1)}) custom-call(f32[8,1024]{1,0:T(8,128)S(1)} %slice_bitcast_fusion.state_ref, f32[2,8,1024]{2,1,0:T(8,128)S(1)} %copy_bitcast_fusion.near_in, f32[2,8,1024]{2,1,0:T(8,128)S(1)} %collective-permute-done.2.far_in, ...), custom_call_target="tpu_custom_call" | custom-call | tf_op jit(solution)/shard_map/forward_first/pallas_call | solution.py:350
  92.7 2.1 %collective-permute-start.18 = (f32[8,1024]{1,0:T(8,128)S(1)}, f32[8,1024]{1,0:T(8,128)S(1)}, u32[]{:S(2)}, u32[]{:S(2)}) collective-permute-start(f32[8,1024]{1,0:T(8,128)S(1)} %get-tuple-element.44), channel_id=1, source_target_pairs={{0,32},{1,33},{2,34},{3,35},{4,36},{5,37},{6,38},{7,39},{8,40},{9,... | collective-permute-start | bytes 98312 | tf_op jit(solution)/shard_map/ppermute | solution.py:359
  94.9 2.5 %flip_trans.1.mats = bf16[4,1024,1024]{2,1,0:T(8,128)(2,1)S(1)} custom-call(bf16[4,8,128,1024]{3,2,1,0:T(8,128)(2,1)S(1)} %get-tuple-element.45.mats_ref), custom_call_target="tpu_custom_call" | custom-call | tf_op jit(solution)/shard_map/flip_trans/pallas_call | solution.py:311
  101.7 0.9 predict.1.pred_ref
  102.6 28.8 %all-gather.7.cloned.1.call-done = bf16[32,128,1024]{2,1,0:T(8,128)(2,1)} async-done(((bf16[2,128,1024]{2,1,0:T(8,128)(2,1)}), bf16[32,128,1024]{2,1,0:T(8,128)(2,1)}) %all-gather.7.cloned.1.call-update) | async-done | bytes 8388624 | tf_op jit(solution)/shard_map/all_gather | solution.py:306
  132.2 4.2 %pack_flip.1.mats = bf16[4,1024,1024]{2,1,0:T(8,128)(2,1)S(1)} custom-call(bf16[2,8,2,128,1024]{4,3,2,1,0:T(8,128)(2,1)} %bitcast.26, f32[8,1024]{1,0:T(8,128)S(1)} %get-tuple-element.63.sent_ref), custom_call_target="tpu_custom_call" | custom-call | tf_op jit(solution)/shard_map/pack_flip/pallas_call | solution.py:373
  140.0 1.3 collective-permute-start.31
  141.3 34.1 %collective-permute-done.31.state_ref = f32[8,1024]{1,0:T(8,128)S(1)} collective-permute-done((f32[8,1024]{1,0:T(8,128)S(1)}, f32[8,1024]{1,0:T(8,128)S(1)}, u32[]{:S(2)}, u32[]{:S(2)}) %collective-permute-start.31) | collective-permute-done | bytes 32800 | tf_op jit(solution)/shard_map/ppermute | solution.py:378
  175.4 1.3 backward.13.smooth_ref
  (106 shorter events, 21.6 us)
Async XLA Ops:
  6.5 79.0 %all-gather.5.cloned.1.call-start = ((), (), s32[]{:S(2)}) async-start(), calls=%async_computation.2 | async-start | bytes 6684672 | tf_op jit(solution)/shard_map/all_gather | solution.py:306
  17.8 113.6 %all-gather.7.cloned.1.call-start = ((), (), s32[]{:S(2)}) async-start(), calls=%async_computation.3 | async-start | bytes 8912896 | tf_op jit(solution)/shard_map/all_gather | solution.py:306
  18.7 9.7 %collective-permute-start = (f32[2,8,16]{2,1,0:T(8,128)S(1)}, f32[2,8,16]{2,1,0:T(8,128)S(1)}, u32[]{:S(2)}, u32[]{:S(2)}) collective-permute-start(f32[2,8,16]{2,1,0:T(8,128)S(1)} %get-tuple-element.77), channel_id=1, source_target_pairs={{0,2},{2,4},{4,6},{6,8},{8,10},{10,12},{12,14},{14,0},{1,3},{3,5},... | collective-permute-start | bytes 3080 | tf_op jit(solution)/shard_map/ppermute | solution.py:33
  20.6 7.8 %collective-permute-start.1 = (f32[2,8,16]{2,1,0:T(8,128)S(1)}, f32[2,8,16]{2,1,0:T(8,128)S(1)}, u32[]{:S(2)}, u32[]{:S(2)}) collective-permute-start(f32[2,8,16]{2,1,0:T(8,128)S(1)} %get-tuple-element.78), channel_id=1, source_target_pairs={{0,14},{2,0},{4,2},{6,4},{8,6},{10,8},{12,10},{14,12},{1,15},{3,1}... | collective-permute-start | bytes 3080 | tf_op jit(solution)/shard_map/ppermute | solution.py:34
  53.3 10.2 %collective-permute-start.3 = (bf16[2,32,1024]{2,1,0:T(8,128)(2,1)S(1)}, bf16[2,32,1024]{2,1,0:T(8,128)(2,1)S(1)}, u32[]{:S(2)}, u32[]{:S(2)}) collective-permute-start(bf16[2,32,1024]{2,1,0:T(8,128)(2,1)S(1)} %slice.37.refs_0_), channel_id=1, source_target_pairs={{0,2},{2,4},{4,6},{6,8},{8,10},{10,12},{12,14},{14,0},{1,3},{3,5},... | collective-permute-start | bytes 393224 | tf_op jit(solution)/shard_map/ppermute | solution.py:318
  54.1 15.3 %collective-permute-start.7 = (bf16[2,32,1024]{2,1,0:T(8,128)(2,1)S(1)}, bf16[2,32,1024]{2,1,0:T(8,128)(2,1)S(1)}, u32[]{:S(2)}, u32[]{:S(2)}) collective-permute-start(bf16[2,32,1024]{2,1,0:T(8,128)(2,1)S(1)} %slice.37.refs_0_), channel_id=1, source_target_pairs={{0,14},{2,0},{4,2},{6,4},{8,6},{10,8},{12,10},{14,12},{1,15},{3,1}... | collective-permute-start | bytes 393224 | tf_op jit(solution)/shard_map/ppermute | solution.py:320
  63.5 9.5 %collective-permute-start.4 = (bf16[2,32,1024]{2,1,0:T(8,128)(2,1)S(1)}, bf16[2,32,1024]{2,1,0:T(8,128)(2,1)S(1)}, u32[]{:S(2)}, u32[]{:S(2)}) collective-permute-start(bf16[2,32,1024]{2,1,0:T(8,128)(2,1)S(1)} %collective-permute-done.3.refs_1_), channel_id=1, source_target_pairs={{0,2},{2,4},{4,6},{6,8},{8,10},{10,12},{12,14},{14,0},{1,3},{3,5},... | collective-permute-start | bytes 393224 | tf_op jit(solution)/shard_map/ppermute | solution.py:318
  64.9 14.5 %all-to-all-start.1 = ((f32[8,3,8,128]{3,2,1,0:T(8,128)}), f32[8,3,8,128]{3,2,1,0:T(8,128)S(1)}, u32[]{:S(2)}, u32[]{:S(2)}) async-start(f32[8,3,8,128]{3,2,1,0:T(8,128)} %broadcast_in_dim.11), calls=%async_computation.1 | async-start | bytes 196608 | tf_op jit(solution)/shard_map/all_to_all | solution.py:28
  69.4 6.0 %collective-permute-start.8 = (bf16[2,32,1024]{2,1,0:T(8,128)(2,1)S(1)}, bf16[2,32,1024]{2,1,0:T(8,128)(2,1)S(1)}, u32[]{:S(2)}, u32[]{:S(2)}) collective-permute-start(bf16[2,32,1024]{2,1,0:T(8,128)(2,1)S(1)} %collective-permute-done.7.refs_7_), channel_id=1, source_target_pairs={{0,14},{2,0},{4,2},{6,4},{8,6},{10,8},{12,10},{14,12},{1,15},{3,1}... | collective-permute-start | bytes 393224 | tf_op jit(solution)/shard_map/ppermute | solution.py:320
  73.1 6.3 %collective-permute-start.5 = (bf16[2,32,1024]{2,1,0:T(8,128)(2,1)S(1)}, bf16[2,32,1024]{2,1,0:T(8,128)(2,1)S(1)}, u32[]{:S(2)}, u32[]{:S(2)}) collective-permute-start(bf16[2,32,1024]{2,1,0:T(8,128)(2,1)S(1)} %collective-permute-done.4.refs_2_), channel_id=1, source_target_pairs={{0,2},{2,4},{4,6},{6,8},{8,10},{10,12},{12,14},{14,0},{1,3},{3,5},... | collective-permute-start | bytes 393224 | tf_op jit(solution)/shard_map/ppermute | solution.py:318
  73.1 6.3 %collective-permute-start.10 = (bf16[2,32,1024]{2,1,0:T(8,128)(2,1)S(1)}, bf16[2,32,1024]{2,1,0:T(8,128)(2,1)S(1)}, u32[]{:S(2)}, u32[]{:S(2)}) collective-permute-start(bf16[2,32,1024]{2,1,0:T(8,128)(2,1)S(1)} %slice.37.refs_0_), channel_id=1, source_target_pairs={{0,16},{16,0},{1,17},{17,1},{2,18},{18,2},{3,19},{19,3},{4,20},{20... | collective-permute-start | bytes 393224 | tf_op jit(solution)/shard_map/ppermute | solution.py:322
  73.1 7.8 %collective-permute-start.11 = (bf16[2,32,1024]{2,1,0:T(8,128)(2,1)S(1)}, bf16[2,32,1024]{2,1,0:T(8,128)(2,1)S(1)}, u32[]{:S(2)}, u32[]{:S(2)}) collective-permute-start(bf16[2,32,1024]{2,1,0:T(8,128)(2,1)S(1)} %collective-permute-done.3.refs_1_), channel_id=1, source_target_pairs={{0,16},{16,0},{1,17},{17,1},{2,18},{18,2},{3,19},{19,3},{4,20},{20... | collective-permute-start | bytes 393224 | tf_op jit(solution)/shard_map/ppermute | solution.py:322
  73.6 7.9 %collective-permute-start.17 = (bf16[2,32,1024]{2,1,0:T(8,128)(2,1)S(1)}, bf16[2,32,1024]{2,1,0:T(8,128)(2,1)S(1)}, u32[]{:S(2)}, u32[]{:S(2)}) collective-permute-start(bf16[2,32,1024]{2,1,0:T(8,128)(2,1)S(1)} %collective-permute-done.7.refs_7_), channel_id=1, source_target_pairs={{0,16},{16,0},{1,17},{17,1},{2,18},{18,2},{3,19},{19,3},{4,20},{20... | collective-permute-start | bytes 393224 | tf_op jit(solution)/shard_map/ppermute | solution.py:322
  75.4 6.6 %collective-permute-start.9 = (bf16[2,32,1024]{2,1,0:T(8,128)(2,1)S(1)}, bf16[2,32,1024]{2,1,0:T(8,128)(2,1)S(1)}, u32[]{:S(2)}, u32[]{:S(2)}) collective-permute-start(bf16[2,32,1024]{2,1,0:T(8,128)(2,1)S(1)} %collective-permute-done.8.refs_6_), channel_id=1, source_target_pairs={{0,14},{2,0},{4,2},{6,4},{8,6},{10,8},{12,10},{14,12},{1,15},{3,1}... | collective-permute-start | bytes 393224 | tf_op jit(solution)/shard_map/ppermute | solution.py:320
  79.4 6.2 %collective-permute-start.6 = (bf16[2,32,1024]{2,1,0:T(8,128)(2,1)S(1)}, bf16[2,32,1024]{2,1,0:T(8,128)(2,1)S(1)}, u32[]{:S(2)}, u32[]{:S(2)}) collective-permute-start(bf16[2,32,1024]{2,1,0:T(8,128)(2,1)S(1)} %collective-permute-done.5.refs_3_), channel_id=1, source_target_pairs={{0,2},{2,4},{4,6},{6,8},{8,10},{10,12},{12,14},{14,0},{1,3},{3,5},... | collective-permute-start | bytes 393224 | tf_op jit(solution)/shard_map/ppermute | solution.py:318
  79.4 2.2 %collective-permute-start.2 = (f32[2,8,1024]{2,1,0:T(8,128)S(1)}, f32[2,8,1024]{2,1,0:T(8,128)S(1)}, u32[]{:S(2)}, u32[]{:S(2)}) collective-permute-start(f32[2,8,1024]{2,1,0:T(8,128)S(1)} %copy_bitcast_fusion.near_in), channel_id=1, source_target_pairs={{0,16},{16,0},{1,17},{17,1},{2,18},{18,2},{3,19},{19,3},{4,20},{20... | collective-permute-start | bytes 196616 | tf_op jit(solution)/shard_map/ppermute | solution.py:336
  80.9 4.7 %collective-permute-start.12 = (bf16[2,32,1024]{2,1,0:T(8,128)(2,1)S(1)}, bf16[2,32,1024]{2,1,0:T(8,128)(2,1)S(1)}, u32[]{:S(2)}, u32[]{:S(2)}) collective-permute-start(bf16[2,32,1024]{2,1,0:T(8,128)(2,1)S(1)} %collective-permute-done.4.refs_2_), channel_id=1, source_target_pairs={{0,16},{16,0},{1,17},{17,1},{2,18},{18,2},{3,19},{19,3},{4,20},{20... | collective-permute-start | bytes 393224 | tf_op jit(solution)/shard_map/ppermute | solution.py:322
  81.5 4.1 %collective-permute-start.16 = (bf16[2,32,1024]{2,1,0:T(8,128)(2,1)S(1)}, bf16[2,32,1024]{2,1,0:T(8,128)(2,1)S(1)}, u32[]{:S(2)}, u32[]{:S(2)}) collective-permute-start(bf16[2,32,1024]{2,1,0:T(8,128)(2,1)S(1)} %collective-permute-done.8.refs_6_), channel_id=1, source_target_pairs={{0,16},{16,0},{1,17},{17,1},{2,18},{18,2},{3,19},{19,3},{4,20},{20... | collective-permute-start | bytes 393224 | tf_op jit(solution)/shard_map/ppermute | solution.py:322
  81.6 4.0 %collective-permute-start.13 = (bf16[2,32,1024]{2,1,0:T(8,128)(2,1)S(1)}, bf16[2,32,1024]{2,1,0:T(8,128)(2,1)S(1)}, u32[]{:S(2)}, u32[]{:S(2)}) collective-permute-start(bf16[2,32,1024]{2,1,0:T(8,128)(2,1)S(1)} %collective-permute-done.5.refs_3_), channel_id=1, source_target_pairs={{0,16},{16,0},{1,17},{17,1},{2,18},{18,2},{3,19},{19,3},{4,20},{20... | collective-permute-start | bytes 393224 | tf_op jit(solution)/shard_map/ppermute | solution.py:322
  82.0 3.6 %collective-permute-start.15 = (bf16[2,32,1024]{2,1,0:T(8,128)(2,1)S(1)}, bf16[2,32,1024]{2,1,0:T(8,128)(2,1)S(1)}, u32[]{:S(2)}, u32[]{:S(2)}) collective-permute-start(bf16[2,32,1024]{2,1,0:T(8,128)(2,1)S(1)} %collective-permute-done.9.refs_5_), channel_id=1, source_target_pairs={{0,16},{16,0},{1,17},{17,1},{2,18},{18,2},{3,19},{19,3},{4,20},{20... | collective-permute-start | bytes 393224 | tf_op jit(solution)/shard_map/ppermute | solution.py:322
  85.6 1.3 collective-permute-start.14
  92.7 4.7 %collective-permute-start.18 = (f32[8,1024]{1,0:T(8,128)S(1)}, f32[8,1024]{1,0:T(8,128)S(1)}, u32[]{:S(2)}, u32[]{:S(2)}) collective-permute-start(f32[8,1024]{1,0:T(8,128)S(1)} %get-tuple-element.44), channel_id=1, source_target_pairs={{0,32},{1,33},{2,34},{3,35},{4,36},{5,37},{6,38},{7,39},{8,40},{9,... | collective-permute-start | bytes 98312 | tf_op jit(solution)/shard_map/ppermute | solution.py:359
  131.5 4.9 %collective-permute-start.25 = (f32[8,1024]{1,0:T(8,128)S(1)}, f32[8,1024]{1,0:T(8,128)S(1)}, u32[]{:S(2)}, u32[]{:S(2)}) collective-permute-start(f32[8,1024]{1,0:T(8,128)S(1)} %get-tuple-element.63.sent_ref), channel_id=1, source_target_pairs={{224,192},{225,193},{226,194},{227,195},{228,196},{229,197},{230,1... | collective-permute-start | bytes 98312 | tf_op jit(solution)/shard_map/ppermute | solution.py:378
  140.0 35.4 %collective-permute-start.31 = (f32[8,1024]{1,0:T(8,128)S(1)}, f32[8,1024]{1,0:T(8,128)S(1)}, u32[]{:S(2)}, u32[]{:S(2)}) collective-permute-start(f32[8,1024]{1,0:T(8,128)S(1)} %get-tuple-element.75), channel_id=1, source_target_pairs={{32,0},{33,1},{34,2},{35,3},{36,4},{37,5},{38,6},{39,7},{40,8},{41... | collective-permute-start | bytes 98312 | tf_op jit(solution)/shard_map/ppermute | solution.py:378
  (13 other events, 44.8 us)
Sparse Core Ops, SparseCore 0:
  17.9 56.0 all-gather.4
  75.9 55.4 all-gather.6
